TPU v7x, 128 devices: a whole 4x4x4 slice. The times are simulated.
128 devices in a mesh: lev: 4 (over x), row: 32 (over y, z, core).
Axes of the slice: x: 4, y: 4, z: 4, core: 2. Of those that a mesh axis runs over, the one named last changes fastest.
Arguments:
- control: float32 [16, 1536, 3072], P('lev', 'row'), may hold values from -6 to 6
- decay_lon: float32 [1536], P('row'), may hold values from 0.5 to 0.99
- decay_lat: float32 [3072], replicated, may hold values from 0.5 to 0.99
- decay_vert: float32 [1536, 3072], P('row'), may hold values from 0.5 to 0.97
Outputs:
- increment: float32 [16, 1536, 3072], P('lev', 'row')
All inputs are finite; a program needn't handle non-finite values.
Results may differ from a plain program's by a relative error of at most 0.002.
Values sent between devices are 32-bit elements; how exact they have to be, the bound alone decides.
A program may use at most 192 MiB of HBM per device.

v0:
```python
import jax
import jax.numpy as jnp
from jax import lax
from jax.sharding import PartitionSpec as P

block_cells = 128


def passed_along(value, axis, by):
    length = lax.axis_size(axis)
    pairs = [(i, i + by) for i in range(length) if 0 <= i + by < length]
    return lax.ppermute(value, axis, pairs)


def sweep_gain(decay):
    sq = decay * decay
    return ((1.0 - sq) ** 7 / (1.0 + 9.0 * sq + 9.0 * sq * sq + sq * sq * sq)) ** 0.25


def state_map(decay, count):
    power = decay**count
    return (
        (count + 1) * power,
        -count * power * decay,
        count * power / decay,
        -(count - 1) * power,
    )


def sweep_triangle(decay, width):
    gain = sweep_gain(decay)
    lag = jnp.arange(width)[:, None] - jnp.arange(width)[None, :]
    lag_pos = jnp.maximum(lag, 0).astype(jnp.float32)
    powers = decay[:, None, None] ** lag_pos[None]
    return jnp.where(lag[None] >= 0, gain[:, None, None] * (lag_pos[None] + 1.0) * powers, 0.0)


def block_forward(field, decay):
    outer, lines, length = field.shape
    count = length // block_cells
    triangle = sweep_triangle(decay, block_cells)
    blocks = field.reshape(outer, lines, count, block_cells)
    local = jnp.einsum("pqbj,qij->pqbi", blocks, triangle, precision=lax.Precision.HIGHEST)
    a11, a12, a21, a22 = state_map(decay, block_cells)

    def advance(state, ends):
        first, second = state
        new_first = a11 * first + a12 * second + ends[0]
        new_second = a21 * first + a22 * second + ends[1]
        return ((new_first, new_second), state)

    ends = (
        jnp.moveaxis(local[..., block_cells - 1], 2, 0),
        jnp.moveaxis(local[..., block_cells - 2], 2, 0),
    )
    zeros = jnp.zeros((outer, lines), jnp.float32)
    _, entering = lax.scan(advance, (zeros, zeros), ends)
    first = jnp.moveaxis(entering[0], 0, 2)
    second = jnp.moveaxis(entering[1], 0, 2)
    pole = decay[:, None]
    coef_one = 2.0 * pole * first - pole * pole * second
    coef_two = pole * first - pole * pole * second
    offsets = jnp.arange(block_cells).astype(jnp.float32)
    decays = decay[:, None] ** offsets[None, :]
    correction = (coef_one[..., None] + coef_two[..., None] * offsets) * decays[None, :, None, :]
    return (local + correction).reshape(outer, lines, length)


def block_filter(field, decay):
    ahead = block_forward(field, decay)
    return jnp.flip(block_forward(jnp.flip(ahead, 2), decay), 2)


def carried(local, decay, carry, reverse):
    count = local.shape[0]
    first, second = carry(decay, count, (local[count - 1], local[count - 2]), reverse)
    coef_one = 2.0 * decay * first - decay * decay * second
    coef_two = decay * first - decay * decay * second
    offsets = jnp.arange(count).astype(jnp.float32).reshape((count,) + (1,) * (local.ndim - 1))
    return local + (coef_one[None] + coef_two[None] * offsets) * decay[None] ** offsets


def chain_forward(data, decay, carry, reverse):
    gain = sweep_gain(decay)

    def step(state, row):
        first, second = state
        value = gain * row + 2.0 * decay * first - decay * decay * second
        return ((value, first), value)

    zeros = jnp.zeros(data.shape[1:], jnp.float32)
    _, local = lax.scan(step, (zeros, zeros), data)
    return carried(local, decay, carry, reverse)


def chain_filter(field, decay, carry):
    ahead = chain_forward(field, decay, carry, False)
    return jnp.flip(chain_forward(jnp.flip(ahead, 0), decay, carry, True), 0)


def full_maps(decay, count):
    return tuple((entry for entry in state_map(decay, count)))


def level_carry(decay, count, ends, reverse):
    maps = full_maps(decay, count)
    offset = -1 if reverse else 1
    state = jnp.zeros((2,) + ends[0].shape, jnp.float32)
    for turn in range(lax.axis_size("lev") - 1):
        first, second = (state[0], state[1])
        leaving = jnp.stack(
            [
                maps[0] * first + maps[1] * second + ends[0],
                maps[2] * first + maps[3] * second + ends[1],
            ]
        )
        state = passed_along(leaving, "lev", offset)
    return (state[0], state[1])


def per_device(control, decay_lon, decay_lat, decay_vert):
    along_lon = block_filter(control, decay_lon)
    columns = jnp.swapaxes(along_lon, 1, 2)
    vertical_poles = jnp.swapaxes(decay_vert, 0, 1)[None]
    columns, vertical_poles = (
        lax.all_to_all(columns, "row", split_axis=1, concat_axis=2, tiled=True),
        lax.all_to_all(vertical_poles, "row", split_axis=1, concat_axis=2, tiled=True),
    )
    col_width = columns.shape[1]
    start = lax.axis_index("row") * col_width
    own_poles = lax.dynamic_slice_in_dim(decay_lat, start, col_width)
    along_lat = block_filter(columns, own_poles)
    filtered = chain_filter(along_lat, vertical_poles[0], level_carry)
    returned = lax.all_to_all(filtered, "row", split_axis=2, concat_axis=1, tiled=True)
    return jnp.swapaxes(returned, 1, 2)


def solution(mesh):
    in_specs = (P("lev", "row", None), P("row"), P(), P("row", None))
    out_specs = P("lev", "row", None)
    return jax.shard_map(
        per_device, mesh=mesh, in_specs=in_specs, out_specs=out_specs, check_vma=False
    )
```

profile of v0, /device:TPU:1, one launch (start us, length us, event | category | flops | bytes accessed | tf_op | source)
XLA Modules:
  0.0 668.1 jit_solution(9069915505886807288)
XLA Ops:
  2.1 13.7 %reduce.1 = f32[3072,48]{1,0:T(8,128)S(1)} reduce(f32[3072,1,48]{2,1,0:T(1,128)S(1)} %bitcast.305, f32[]{:T(128)} %broadcast.496), dimensions={1}, to_apply=%bitcast.258.reduce_sub_computation | reduce | bytes 1179652
  18.1 9.9 %all-to-all-start.1 = ((f32[32,1,4608]{2,1,0:T(1,128)}), f32[32,1,4608]{2,1,0:T(1,128)S(1)}, u32[]{:S(2)}, u32[]{:S(2)}) async-start(f32[32,1,4608]{2,1,0:T(1,128)} %reshape.294), calls=%async_computation.1 | async-start | bytes 1179648 | tf_op jit(solution)/shard_map/all_to_all | solution.py:127
  30.3 9.5 %fusion.36 = f32[4,48,24,128]{3,2,0,1:T(8,128)S(1)} fusion(f32[128,128]{1,0:T(8,128)S(1)} %maximum_convert_fusion, f32[48]{0:T(128)S(1)} %copy-done.9, f32[128,128]{1,0:T(8,128)S(1)} %broadcast_add_fusion, f32[48]{0:T(128)S(1)} %get-tuple-element.950, pred[128,128]{1,0:T(8,128)(4,1)S(1)} %fusion.68, f32[4,48,24,128]{3,2,1,0:T(8,128)S(1)} %bitcast.309), kind=kOutput, calls=%fused_computation.65 | convolution fusion | flops 908328960 | bytes 4866432 | tf_op jit(solution)/shard_map/pqbj,qij->pqbi/dot_general | solution.py:43
  39.8 3.5 fusion.98
  56.5 10.0 %rev.21 = f32[4,48,3072]{2,0,1:T(4,128)} reverse(f32[4,48,3072]{2,0,1:T(4,128)S(1)} %reshape.281), dimensions={2} | reverse | bytes 4718592 | tf_op jit(solution)/shard_map/jit(_flip)/rev | solution.py:71
  66.5 4.1 reshape.282
  70.6 11.1 %fusion.41 = f32[4,48,24,128]{3,2,0,1:T(8,128)S(1)} fusion(f32[4,48,24,128]{3,2,0,1:T(8,128)} %reshape.282, f32[128,128]{1,0:T(8,128)S(1)} %maximum_convert_fusion, f32[48]{0:T(128)S(1)} %copy-done.9, f32[128,128]{1,0:T(8,128)S(1)} %broadcast_add_fusion, f32[48]{0:T(128)S(1)} %get-tuple-element.950, pred[128,128]{1,0:T(8,128)(4,1)S(1)} %fusion.68), kind=kOutput, calls=%fused_computation.66 | convolution fusion | flops 908328960 | bytes 4866432 | tf_op jit(solution)/shard_map/pqbj,qij->pqbi/dot_general | solution.py:43
  81.7 3.5 fusion.97
  95.7 5.6 copy.172
  101.3 6.9 %fusion.105 = f32[3072,4,48]{2,1,0:T(4,128)} fusion(f32[4,48,3072]{1,0,2:T(4,128)} %bitcast.300), kind=kLoop, calls=%fused_computation.195 | loop fusion | bytes 4718592
  108.2 9.3 %reshape.292 = f32[32,1,18432]{2,1,0:T(1,128)} reshape(f32[3072,4,48]{2,1,0:T(4,128)} %fusion.105) | data formatting | bytes 4718592
  117.5 7.4 %all-to-all-start = ((f32[32,1,18432]{2,1,0:T(1,128)}), f32[32,1,18432]{2,1,0:T(1,128)}, u32[]{:S(2)}, u32[]{:S(2)}) async-start(f32[32,1,18432]{2,1,0:T(1,128)} %reshape.292), calls=%async_computation | async-start | bytes 4718592 | tf_op jit(solution)/shard_map/all_to_all | solution.py:126
  136.9 19.2 %all-to-all-done = f32[32,1,18432]{2,1,0:T(1,128)} async-done(((f32[32,1,18432]{2,1,0:T(1,128)}), f32[32,1,18432]{2,1,0:T(1,128)}, u32[]{:S(2)}, u32[]{:S(2)}) %all-to-all-start) | async-done | bytes 2359328 | tf_op jit(solution)/shard_map/all_to_all | solution.py:126
  156.1 9.3 %reduce = f32[32,18432]{1,0:T(8,128)} reduce(f32[32,1,18432]{2,1,0:T(1,128)} %all-to-all-done, f32[]{:T(128)} %broadcast.496), dimensions={1}, to_apply=%all_to_all.35.reduce_sub_computation | reduce | bytes 4718596 | tf_op jit(solution)/shard_map/all_to_all | solution.py:126
  165.4 8.6 %reshape.293 = f32[3072,4,48]{2,1,0:T(4,128)} reshape(f32[32,18432]{1,0:T(8,128)} %reduce) | data formatting | bytes 4718592
  174.0 6.8 %copy.174 = f32[4,32,96,48]{2,3,1,0:T(8,128)} copy(f32[4,32,96,48]{3,0,2,1:T(4,128)} %bitcast.301) | data formatting | bytes 4718592 | tf_op jit(solution)/shard_map/all_to_all | solution.py:126
  180.9 5.3 copy.123
  186.2 19.7 %fusion.28 = f32[4,96,12,128]{3,2,0,1:T(8,128)S(1)} fusion(f32[4,96,12,128]{3,2,0,1:T(8,128)} %copy.123, f32[128,128]{1,0:T(8,128)S(1)} %maximum_convert_fusion, f32[96]{0:T(128)S(1)} %copy-done.13, f32[128,128]{1,0:T(8,128)S(1)} %broadcast_add_fusion, f32[96]{0:T(128)S(1)} %copy-done.16, pred[128,128]{1,0:T(8,128)(4,1)S(1)} %fusion.68), kind=kOutput, calls=%fused_computation.63 | convolution fusion | flops 910688256 | bytes 4866816 | tf_op jit(solution)/shard_map/pqbj,qij->pqbi/dot_general | solution.py:43
  205.8 4.3 fusion.96
  217.5 5.1 multiply_add_fusion.1
  222.5 4.3 reshape.290
  226.8 3.8 copy.175
  230.7 24.9 %rev.23 = f32[4,96,1536]{2,1,0:T(8,128)} reverse(f32[4,96,1536]{2,1,0:T(8,128)} %copy.175), dimensions={2} | reverse | bytes 4718592 | tf_op jit(solution)/shard_map/jit(_flip)/rev | solution.py:71
  255.6 3.9 reshape.286
  259.5 19.9 %fusion.31 = f32[4,96,12,128]{3,2,0,1:T(8,128)S(1)} fusion(f32[4,96,12,128]{3,2,1,0:T(8,128)} %reshape.286, f32[128,128]{1,0:T(8,128)S(1)} %maximum_convert_fusion, f32[96]{0:T(128)S(1)} %copy-done.13, f32[128,128]{1,0:T(8,128)S(1)} %broadcast_add_fusion, f32[96]{0:T(128)S(1)} %copy-done.16, pred[128,128]{1,0:T(8,128)(4,1)S(1)} %fusion.68), kind=kOutput, calls=%fused_computation.64 | convolution fusion | flops 910688256 | bytes 4866816 | tf_op jit(solution)/shard_map/pqbj,qij->pqbi/dot_general | solution.py:43
  279.4 4.3 fusion.95
  290.9 5.1 multiply_add_fusion
  296.0 4.3 reshape.291
  300.2 3.9 copy.176
  304.1 25.1 %rev.24 = f32[4,96,1536]{2,1,0:T(8,128)} reverse(f32[4,96,1536]{2,1,0:T(8,128)} %copy.176), dimensions={2} | reverse | bytes 4718592 | tf_op jit(solution)/shard_map/jit(_flip)/rev | solution.py:71
  331.0 11.0 %while.104 = (s32[]{:T(128)}, f32[96,1536]{1,0:T(8,128)}, f32[96,1536]{1,0:T(8,128)S(1)}, f32[4,96,1536]{2,1,0:T(8,128)}, f32[4,96,1536]{2,1,0:T(8,128)}, /*inde...) while((s32[]{:T(128)}, f32[96,1536]{1,0:T(8,128)}, ...), condition=%wide.region_9.10_spmd.clone, body=%wide.region_8.9_spmd.clone.sunk | while | flops 1032195 | bytes 5309039 | solution.py:92
  341.9 3.4 copy.140
  354.6 24.4 %collective-permute-done = f32[2,96,1536]{2,1,0:T(8,128)S(1)} collective-permute-done((f32[2,96,1536]{2,1,0:T(8,128)}, f32[2,96,1536]{2,1,0:T(8,128)S(1)}, u32[]{:S(2)}, u32[]{:S(2)}) %collective-permute-start) | collective-permute-done | bytes 1179680 | tf_op jit(solution)/shard_map/ppermute | solution.py:12
  389.9 4.1 collective-permute-start.1
  394.0 23.7 %collective-permute-done.1 = f32[2,96,1536]{2,1,0:T(8,128)S(1)} collective-permute-done((f32[2,96,1536]{2,1,0:T(8,128)}, f32[2,96,1536]{2,1,0:T(8,128)S(1)}, u32[]{:S(2)}, u32[]{:S(2)}) %collective-permute-start.1) | collective-permute-done | bytes 1179680 | tf_op jit(solution)/shard_map/ppermute | solution.py:12
  428.5 5.1 collective-permute-start.2
  433.6 4.5 copy.151
  438.1 17.2 %collective-permute-done.2 = f32[2,96,1536]{2,1,0:T(8,128)} collective-permute-done((f32[2,96,1536]{2,1,0:T(8,128)}, f32[2,96,1536]{2,1,0:T(8,128)}, u32[]{:S(2)}, u32[]{:S(2)}) %collective-permute-start.2) | collective-permute-done | bytes 1179680 | tf_op jit(solution)/shard_map/ppermute | solution.py:12
  463.3 8.0 %fusion.8 = f32[4,96,1536]{1,0,2:T(4,128)} fusion(f32[4,96,1536]{1,0,2:T(4,128)S(1)} %copy-done.4, f32[96,1536]{0,1:T(8,128)S(1)} %bitcast.298, f32[4]{0:T(128)S(1)} %iota_convert_fusion, f32[96,1536]{0,1:T(8,128)S(1)} %bitcast.307, f32[96,1536]{0,1:T(8,128)S(1)} %get-tuple-element.913), kind=kLoop, calls=%fused_computation.38 | loop fusion | flops 2359296 | bytes 6488080 | tf_op jit(solution)/shard_map/add | solution.py:80
  471.3 9.0 %rev.25 = f32[4,96,1536]{1,0,2:T(4,128)} reverse(f32[4,96,1536]{1,0,2:T(4,128)} %fusion.8), dimensions={0} | reverse | bytes 4718592 | tf_op jit(solution)/shard_map/jit(_flip)/rev | solution.py:98
  480.4 4.7 copy.152
  486.7 11.0 %while.105 = (s32[]{:T(128)}, f32[96,1536]{1,0:T(8,128)}, f32[96,1536]{1,0:T(8,128)S(1)}, f32[4,96,1536]{2,1,0:T(8,128)}, f32[4,96,1536]{2,1,0:T(8,128)}, /*inde...) while((s32[]{:T(128)}, f32[96,1536]{1,0:T(8,128)}, ...), condition=%wide.region_11.12_spmd.clone, body=%wide.region_10.11_spmd.clone.sunk | while | flops 1032195 | bytes 5309039 | solution.py:92
  504.7 25.4 %collective-permute-done.3 = f32[2,96,1536]{2,1,0:T(8,128)S(1)} collective-permute-done((f32[2,96,1536]{2,1,0:T(8,128)S(1)}, f32[2,96,1536]{2,1,0:T(8,128)S(1)}, u32[]{:S(2)}, u32[]{:S(2)}) %collective-permute-start.3) | collective-permute-done | bytes 1179680 | tf_op jit(solution)/shard_map/ppermute | solution.py:12
  534.7 23.5 %collective-permute-done.4 = f32[2,96,1536]{2,1,0:T(8,128)S(1)} collective-permute-done((f32[2,96,1536]{2,1,0:T(8,128)S(1)}, f32[2,96,1536]{2,1,0:T(8,128)S(1)}, u32[]{:S(2)}, u32[]{:S(2)}) %collective-permute-start.4) | collective-permute-done | bytes 1179680 | tf_op jit(solution)/shard_map/ppermute | solution.py:12
  568.9 20.3 %collective-permute-done.5 = f32[2,96,1536]{2,1,0:T(8,128)} collective-permute-done((f32[2,96,1536]{2,1,0:T(8,128)}, f32[2,96,1536]{2,1,0:T(8,128)}, u32[]{:S(2)}, u32[]{:S(2)}) %collective-permute-start.5) | collective-permute-done | bytes 1179680 | tf_op jit(solution)/shard_map/ppermute | solution.py:12
  593.0 8.0 %fusion.9 = f32[4,96,1536]{1,0,2:T(4,128)} fusion(f32[4,96,1536]{1,0,2:T(4,128)S(1)} %copy-done.3, f32[96,1536]{0,1:T(8,128)S(1)} %bitcast.306, f32[96,1536]{0,1:T(8,128)S(1)} %get-tuple-element.911, f32[96,1536]{0,1:T(8,128)S(1)} %bitcast.299, f32[4]{0:T(128)S(1)} %iota_convert_fusion), kind=kLoop, calls=%fused_computation.39 | loop fusion | flops 2359296 | bytes 6488080 | tf_op jit(solution)/shard_map/add | solution.py:80
  601.0 7.6 %rev.26 = f32[4,96,1536]{1,0,2:T(4,128)S(1)} reverse(f32[4,96,1536]{1,0,2:T(4,128)} %fusion.9), dimensions={0} | reverse | bytes 4718592 | tf_op jit(solution)/shard_map/jit(_flip)/rev | solution.py:98
  608.6 55.3 %all_to_all.48 = f32[4,96,1536]{1,0,2:T(4,128)S(1)} all-to-all(f32[4,96,1536]{1,0,2:T(4,128)S(1)} %rev.26), channel_id=1, replica_groups=mesh['lev'=4,'row'=32] {'row'}, dimensions={2} | all-to-all | bytes 4718592 | tf_op jit(solution)/shard_map/all_to_all | solution.py:134
  (354 shorter events, 153.5 us)
Async XLA Ops:
  2.1 26.1 %copy-start.9 = (f32[48]{0:T(128)S(1)}, f32[48]{0:T(128)}, u32[]{:S(2)}) copy-start(f32[48]{0:T(128)} %param.17) | copy-start | bytes 580
  18.1 99.3 %all-to-all-start.1 = ((f32[32,1,4608]{2,1,0:T(1,128)}), f32[32,1,4608]{2,1,0:T(1,128)S(1)}, u32[]{:S(2)}, u32[]{:S(2)}) async-start(f32[32,1,4608]{2,1,0:T(1,128)} %reshape.294), calls=%async_computation.1 | async-start | bytes 1179648 | tf_op jit(solution)/shard_map/all_to_all | solution.py:127
  28.1 99.3 %copy-start.10 = (f32[128]{0:T(128)}, f32[128]{0:T(128)S(1)}, u32[]{:S(2)}) copy-start(f32[128]{0:T(128)S(1)} %iota_convert_fusion.1) | copy-start | bytes 1540
  117.5 38.6 %all-to-all-start = ((f32[32,1,18432]{2,1,0:T(1,128)}), f32[32,1,18432]{2,1,0:T(1,128)}, u32[]{:S(2)}, u32[]{:S(2)}) async-start(f32[32,1,18432]{2,1,0:T(1,128)} %reshape.292), calls=%async_computation | async-start | bytes 4718592 | tf_op jit(solution)/shard_map/all_to_all | solution.py:126
  126.3 7.1 %copy-start.12 = (f32[96]{0:T(128)}, f32[96]{0:T(128)S(1)}, u32[]{:S(2)}) copy-start(f32[96]{0:T(128)S(1)} %get-tuple-element.870) | copy-start | bytes 1156
  180.9 5.3 copy-start.13
  180.9 5.3 copy-start.16
  205.8 4.4 copy-start.1
  210.2 6.2 copy-start.5
  210.2 6.2 copy-start.6
  210.2 6.2 copy-start.7
  210.2 6.2 copy-start.8
  210.2 6.9 %copy-start.14 = (f32[96]{0:T(128)S(1)}, f32[96]{0:T(128)}, u32[]{:S(2)}) copy-start(f32[96]{0:T(128)} %get-tuple-element.943) | copy-start | bytes 1156
  210.2 6.9 %copy-start.15 = (f32[96]{0:T(128)S(1)}, f32[96]{0:T(128)}, u32[]{:S(2)}) copy-start(f32[96]{0:T(128)} %get-tuple-element.869) | copy-start | bytes 1156
  210.2 7.2 %copy-start.11 = (f32[128]{0:T(128)S(1)}, f32[128]{0:T(128)}, u32[]{:S(2)}) copy-start(f32[128]{0:T(128)} %copy-done.10) | copy-start | bytes 1540
  279.4 4.4 copy-start
  351.2 27.8 %collective-permute-start = (f32[2,96,1536]{2,1,0:T(8,128)}, f32[2,96,1536]{2,1,0:T(8,128)S(1)}, u32[]{:S(2)}, u32[]{:S(2)}) collective-permute-start(f32[2,96,1536]{2,1,0:T(8,128)} %copy.142), channel_id=1, source_target_pairs={{0,32},{32,64},{64,96},{1,33},{33,65},{65,97},{2,34},{34,66},{66,9... | collective-permute-start | bytes 3538952 | tf_op jit(solution)/shard_map/ppermute | solution.py:12
  389.9 27.7 %collective-permute-start.1 = (f32[2,96,1536]{2,1,0:T(8,128)}, f32[2,96,1536]{2,1,0:T(8,128)S(1)}, u32[]{:S(2)}, u32[]{:S(2)}) collective-permute-start(f32[2,96,1536]{2,1,0:T(8,128)} %copy.145), channel_id=1, source_target_pairs={{0,32},{32,64},{64,96},{1,33},{33,65},{65,97},{2,34},{34,66},{66,9... | collective-permute-start | bytes 3538952 | tf_op jit(solution)/shard_map/ppermute | solution.py:12
  428.5 26.8 %collective-permute-start.2 = (f32[2,96,1536]{2,1,0:T(8,128)}, f32[2,96,1536]{2,1,0:T(8,128)}, u32[]{:S(2)}, u32[]{:S(2)}) collective-permute-start(f32[2,96,1536]{2,1,0:T(8,128)} %copy.148), channel_id=1, source_target_pairs={{0,32},{32,64},{64,96},{1,33},{33,65},{65,97},{2,34},{34,66},{66,9... | collective-permute-start | bytes 3538952 | tf_op jit(solution)/shard_map/ppermute | solution.py:12
  461.2 2.1 copy-start.4
  503.4 26.7 %collective-permute-start.3 = (f32[2,96,1536]{2,1,0:T(8,128)S(1)}, f32[2,96,1536]{2,1,0:T(8,128)S(1)}, u32[]{:S(2)}, u32[]{:S(2)}) collective-permute-start(f32[2,96,1536]{2,1,0:T(8,128)S(1)} %copy.158), channel_id=1, source_target_pairs={{32,0},{64,32},{96,64},{33,1},{65,33},{97,65},{34,2},{66,34},{98,6... | collective-permute-start | bytes 3538952 | tf_op jit(solution)/shard_map/ppermute | solution.py:12
  533.1 25.1 %collective-permute-start.4 = (f32[2,96,1536]{2,1,0:T(8,128)S(1)}, f32[2,96,1536]{2,1,0:T(8,128)S(1)}, u32[]{:S(2)}, u32[]{:S(2)}) collective-permute-start(f32[2,96,1536]{2,1,0:T(8,128)S(1)} %copy.161), channel_id=1, source_target_pairs={{32,0},{64,32},{96,64},{33,1},{65,33},{97,65},{34,2},{66,34},{98,6... | collective-permute-start | bytes 3538952 | tf_op jit(solution)/shard_map/ppermute | solution.py:12
  560.6 5.5 copy-start.2
  564.8 24.4 %collective-permute-start.5 = (f32[2,96,1536]{2,1,0:T(8,128)}, f32[2,96,1536]{2,1,0:T(8,128)}, u32[]{:S(2)}, u32[]{:S(2)}) collective-permute-start(f32[2,96,1536]{2,1,0:T(8,128)} %copy.164), channel_id=1, source_target_pairs={{32,0},{64,32},{96,64},{33,1},{65,33},{97,65},{34,2},{66,34},{98,6... | collective-permute-start | bytes 3538952 | tf_op jit(solution)/shard_map/ppermute | solution.py:12
  591.1 1.9 copy-start.3
where the time goes:
time: 681 us; the launch traced here: 668 us
  local copies, waits for them, and re-layouts  258 us (38%)
  waiting for transfers between devices  154 us (23%)
  other arithmetic  103 us (15%)
  matrix products  60.2 us (9%)
  blocking collectives  55.3 us (8%)
  starting transfers between devices  33.9 us (5%)
    ppermute x6, waiting for transfers between devices, passed_along(): return lax.ppermute(value, axis, pairs)  135 us
    dot_general x4, matrix products, block_forward(): jnp.einsum('pqbj,qij->pqbi', blocks, triangle, precision=lax.Precision.HI...  60.2 us
    rev x3, local copies, waits for them, and re-layouts, block_filter(): return jnp.flip(block_forward(jnp.flip(ahead, 2), decay), 2)  60 us
    all_to_all x1, blocking collectives, per_device(): lax.all_to_all(filtered, 'row', split_axis=2, concat_axis=1, tiled=True)  55.3 us
    unnamed x57, local copies, waits for them, and re-layouts  55.2 us
    slice x8, local copies, waits for them, and re-layouts, block_forward(): local[..., block_cells - 2]  27.3 us
    reshape x6, local copies, waits for them, and re-layouts, block_forward(): return (local + correction).reshape(outer, lines, length)  24.6 us
    dynamic_update_slice x8, other arithmetic, chain_forward(): _, local = lax.scan(step, (zeros, zeros), data)  21.9 us
  transfers between devices with their start and end apart: 8, of which 7 were waited for; matrix products, arithmetic and copies ran while one was open for 16% of the time, Pallas kernels for 0%

commit v1 on v0

v1 whole, which is shorter than its diff:
```python
import functools

import jax
import jax.numpy as jnp
from jax import lax
from jax.experimental import pallas as pl
from jax.experimental.pallas import tpu as pltpu
from jax.sharding import PartitionSpec as P

MESH = pl.DeviceIdType.MESH

LANES = 128
SEG = 24
ROWS = 48
LEV = 4
LINES = LEV * ROWS
BG = SEG // 8
NR = 32
MSG = 16
JC = 6
NJ = ROWS // JC
NCH = BG * NJ
CH = 2 * JC * 8
LAG = 2


def gain_sq(r):
    q = r * r
    a = (1.0 - r) * (1.0 + r)
    a2 = a * a
    a4 = a2 * a2
    return jnp.sqrt(a4 * a2 * a / (1.0 + q * (9.0 + q * (9.0 + q))))


def sums_double(q, n, qn, s0, s1, s2):
    return (
        s0 + qn * s0,
        s1 + qn * (s1 + n * s0),
        s2 + qn * (s2 + (2.0 * n) * s1 + (n * n) * s0),
    )


def sums(q, base, doublings):
    s0 = jnp.ones_like(q)
    s1 = jnp.ones_like(q)
    s2 = jnp.ones_like(q)
    qn = q
    for t in range(1, base):
        s0 = s0 + qn
        s1 = s1 + (t + 1.0) * qn
        s2 = s2 + ((t + 1.0) * (t + 1.0)) * qn
        qn = qn * q
    n = float(base)
    for _ in range(doublings):
        s0, s1, s2 = sums_double(q, n, qn, s0, s1, s2)
        qn = qn * qn
        n = 2.0 * n
    return s0, s1, s2


def power(r, base, doublings):
    p = r
    for _ in range(base - 1):
        p = p * r
    for _ in range(doublings):
        p = p * p
    return p


def kernel(ctrl, dlon, dlat, dvert, out, X, Y, Z, PV, EU, ED, EV, EW,
           SB, RB, RP, CB, SR, SL, FL, FR,
           in_sem, pv_sem, out_sem, s1_sem, r1_sem, s2_sem, r2_sem,
           sr_sem, sl_sem, fl_sem, fr_sem):
    lev = lax.axis_index("lev")
    me = lax.axis_index("row")
    barrier = pltpu.get_barrier_semaphore()

    def in_copy(b):
        return pltpu.make_async_copy(
            ctrl.at[:, pl.ds(pl.multiple_of(b * LANES, LANES), LANES)],
            X.at[pl.ds(pl.multiple_of(b * LINES, 8), LINES), :], in_sem.at[b])

    def pv_copy(b):
        return pltpu.make_async_copy(
            dvert.at[:, pl.ds(pl.multiple_of(b * LANES, LANES), LANES)],
            PV.at[pl.ds(pl.multiple_of(b * ROWS, 8), ROWS), :], pv_sem.at[b])

    def out_copy(b):
        return pltpu.make_async_copy(
            X.at[pl.ds(pl.multiple_of(b * LINES, 8), LINES), :],
            out.at[:, pl.ds(pl.multiple_of(b * LANES, LANES), LANES)], out_sem.at[b])

    def loop(n, body):
        def step(i, carry):
            body(i)
            return carry
        lax.fori_loop(0, n, step, 0)

    loop(SEG, lambda b: in_copy(b).start())
    loop(SEG, lambda b: pv_copy(b).start())

    def greet(i):
        pl.semaphore_signal(barrier, inc=1, device_id=(lev, lax.rem(me + i + 1, NR)), device_id_type=MESH)
    loop(NR - 1, greet)

    @pl.when(lev > 0)
    def _():
        pl.semaphore_signal(barrier, inc=1, device_id=(lev - 1, me), device_id_type=MESH)

    @pl.when(lev < 3)
    def _():
        pl.semaphore_signal(barrier, inc=1, device_id=(lev + 1, me), device_id_type=MESH)

    X[pl.ds(SEG * LINES, 32), :] = jnp.zeros((32, LANES), jnp.float32)

    def lon_in(b):
        in_copy(b).wait()
    loop(SEG, lon_in)

    def turn_in(b):
        for g in range(2):
            tile = X[pl.ds(pl.multiple_of(b * LINES + g * 96, 8), LANES), :]
            Y[pl.ds(g * LANES * SEG + b, LANES, stride=SEG), :] = tile.T
    loop(SEG, turn_in)

    r = dlon[0:8, :]
    zero = jnp.zeros((8, LANES), jnp.float32)
    one = jnp.ones((8, LANES), jnp.float32)
    chains = [(g, bg) for g in range(2) for bg in range(BG)]

    def at_lon(g, bg, l):
        return pl.ds(pl.multiple_of((g * LANES + l) * SEG + bg * 8, 8), 8)

    def lon_ends(l, state):
        p, pp, rest = state
        new = []
        for i, (g, bg) in enumerate(chains):
            u, d, v, w = rest[i]
            d = r * d + Y[at_lon(g, bg, l), :]
            u = r * u + d
            new.append((u, d, v + pp * u, w + p * u))
        p = r * p
        return (p, r * pp + p, tuple(new))

    init = (one, one, tuple((zero, zero, zero, zero) for _ in chains))
    _, _, ends = lax.fori_loop(0, LANES, lon_ends, init, unroll=2)
    for i, (g, bg) in enumerate(chains):
        at = pl.ds(g * SEG + bg * 8, 8)
        EU[at, :], ED[at, :], EV[at, :], EW[at, :] = ends[i]

    r2 = dlon[0:2, :]
    s0, s1, s2 = sums(r2 * r2, 1, 7)
    rn = power(r2, 1, 7)
    n = float(LANES)
    z2 = jnp.zeros((2, LANES), jnp.float32)

    def lon_fwd(b, state):
        u, d = state
        at = pl.ds(b, 2, stride=SEG)
        eu, ed = EU[at, :], ED[at, :]
        EU[at, :] = u
        ED[at, :] = d
        return (rn * (u + n * d) + eu, rn * d + ed)
    lax.fori_loop(0, SEG, lon_fwd, (z2, z2))

    def lon_bwd(i, state):
        v, w = state
        at = pl.ds(SEG - 1 - i, 2, stride=SEG)
        u, d = EU[at, :], ED[at, :]
        ev = EV[at, :] + r2 * (s1 * u + s2 * d)
        ew = EW[at, :] + r2 * (s0 * u + s1 * d)
        EV[at, :] = v
        EW[at, :] = w
        return (rn * (v + n * w) + ev, rn * w + ew)
    lax.fori_loop(0, SEG, lon_bwd, (z2, z2))

    def lon_ahead(l, state):
        new = []
        for i, (g, bg) in enumerate(chains):
            u, d = state[i]
            d = r * d + Y[at_lon(g, bg, l), :]
            u = r * u + d
            Y[at_lon(g, bg, l), :] = u
            new.append((u, d))
        return tuple(new)

    start = tuple((EU[pl.ds(g * SEG + bg * 8, 8), :], ED[pl.ds(g * SEG + bg * 8, 8), :]) for g, bg in chains)
    lax.fori_loop(0, LANES, lon_ahead, start, unroll=2)

    g_lon = gain_sq(r)

    def lon_back(i, state):
        l = LANES - 1 - i
        new = []
        for k, (g, bg) in enumerate(chains):
            v, w = state[k]
            w = r * w + Y[at_lon(g, bg, l), :]
            v = r * v + w
            Y[at_lon(g, bg, l), :] = v * g_lon
            new.append((v, w))
        return tuple(new)

    start = tuple((EV[pl.ds(g * SEG + bg * 8, 8), :], EW[pl.ds(g * SEG + bg * 8, 8), :]) for g, bg in chains)
    lax.fori_loop(0, LANES, lon_back, start, unroll=2)

    def turn_out(b):
        for g in range(2):
            tile = Y[pl.ds(g * LANES * SEG + b, LANES, stride=SEG), :].T
            for k in range(2):
                Z[pl.ds((2 * g + k) * ROWS * SEG + b, ROWS, stride=SEG), :] = tile[k * ROWS:(k + 1) * ROWS, :]
    loop(SEG, turn_out)

    def at_lat(k, j, bg):
        return pl.ds(pl.multiple_of((k * ROWS + j) * SEG + bg * 8, 8), 8)

    loop(NR, lambda i: SB.__setitem__((pl.ds(pl.multiple_of(i * MSG, 8), 8), slice(None)), zero))
    loop(NR, lambda i: SB.__setitem__((pl.ds(pl.multiple_of(i * MSG + 8, 8), 8), slice(None)), zero))
    for bg in range(BG):
        rl = dlat[bg * 8:(bg + 1) * 8, :]

        def lat_ends(j, state, rl=rl, bg=bg):
            p, pp, rest = state
            new = []
            for k in range(LEV):
                u, d, v, w = rest[k]
                d = rl * d + Z[at_lat(k, j, bg), :]
                u = rl * u + d
                new.append((u, d, v + pp * u, w + p * u))
            p = rl * p
            return (p, rl * pp + p, tuple(new))

        init = (one, one, tuple((zero, zero, zero, zero) for _ in range(LEV)))
        _, _, ends = lax.fori_loop(0, ROWS, lat_ends, init, unroll=2)
        for k in range(LEV):
            for val in range(4):
                SB[pl.ds(k * 8 * MSG + val * 4 + bg, 8, stride=MSG), :] = ends[k][val]

    neighbours = (lev > 0).astype(jnp.int32) + (lev < 3).astype(jnp.int32)
    pl.semaphore_wait(barrier, NR - 1 + neighbours)

    def slot(ref, i):
        return ref.at[pl.ds(pl.multiple_of(i * MSG, 8), MSG), :]

    def exchange(src, dst, ssem, rsem):
        def send(i):
            p = lax.rem(me + i + 1, NR)
            pltpu.make_async_remote_copy(
                src_ref=slot(src, p), dst_ref=slot(dst, me), send_sem=ssem.at[p], recv_sem=rsem.at[me],
                device_id=(lev, p), device_id_type=MESH).start()
        loop(NR - 1, send)
        at = pl.ds(pl.multiple_of(me * MSG, 8), MSG)
        dst[at, :] = src[at, :]

        def get(i):
            p = lax.rem(me + i + 1, NR)
            pltpu.make_async_remote_copy(
                src_ref=slot(src, p), dst_ref=slot(dst, p), send_sem=ssem.at[p], recv_sem=rsem.at[p],
                device_id=(lev, p), device_id_type=MESH).wait_recv()
        loop(NR - 1, get)

    def sent(src, dst, ssem, rsem):
        def one_sent(i):
            p = lax.rem(me + i + 1, NR)
            pltpu.make_async_remote_copy(
                src_ref=slot(src, p), dst_ref=slot(dst, me), send_sem=ssem.at[p], recv_sem=rsem.at[me],
                device_id=(lev, p), device_id_type=MESH).wait_send()
        loop(NR - 1, one_sent)

    exchange(SB, RB, s1_sem, r1_sem)

    ro = dlat[pl.ds(lax.rem(me, 8), 4, stride=8), :]
    o0, o1, o2 = sums(ro * ro, 3, 4)
    on = power(ro, 3, 4)
    m = float(ROWS)
    z4 = jnp.zeros((4, LANES), jnp.float32)

    def at_msg(s, val):
        return pl.ds(pl.multiple_of(s * MSG + val * 4, 4), 4)

    def own_fwd(s, state):
        u, d = state
        RP[at_msg(s, 0), :] = u
        RP[at_msg(s, 1), :] = d
        return (on * (u + m * d) + RB[at_msg(s, 0), :], on * d + RB[at_msg(s, 1), :])
    lax.fori_loop(0, NR, own_fwd, (z4, z4))

    def own_bwd(i, state):
        v, w = state
        s = NR - 1 - i
        u, d = RP[at_msg(s, 0), :], RP[at_msg(s, 1), :]
        RP[at_msg(s, 2), :] = v
        RP[at_msg(s, 3), :] = w
        ev = RB[at_msg(s, 2), :] + ro * (o1 * u + o2 * d)
        ew = RB[at_msg(s, 3), :] + ro * (o0 * u + o1 * d)
        return (on * (v + m * w) + ev, on * w + ew)
    lax.fori_loop(0, NR, own_bwd, (z4, z4))

    exchange(RP, CB, s2_sem, r2_sem)

    for bg in range(BG):
        rl = dlat[bg * 8:(bg + 1) * 8, :]
        g_lat = gain_sq(rl)

        def come(k, val, bg=bg):
            return CB[pl.ds(k * 8 * MSG + val * 4 + bg, 8, stride=MSG), :]

        def lat_ahead(j, state, rl=rl, bg=bg):
            new = []
            for k in range(LEV):
                u, d = state[k]
                d = rl * d + Z[at_lat(k, j, bg), :]
                u = rl * u + d
                Z[at_lat(k, j, bg), :] = u
                new.append((u, d))
            return tuple(new)
        lax.fori_loop(0, ROWS, lat_ahead, tuple((come(k, 0), come(k, 1)) for k in range(LEV)), unroll=2)

        def lat_back(i, state, rl=rl, bg=bg, g_lat=g_lat):
            j = ROWS - 1 - i
            new = []
            for k in range(LEV):
                v, w = state[k]
                w = rl * w + Z[at_lat(k, j, bg), :]
                v = rl * v + w
                Z[at_lat(k, j, bg), :] = v * g_lat
                new.append((v, w))
            return tuple(new)
        lax.fori_loop(0, ROWS, lat_back, tuple((come(k, 2), come(k, 3)) for k in range(LEV)), unroll=2)

    loop(SEG, lambda b: pv_copy(b).wait())

    def chunk(ref, c):
        return ref.at[pl.ds(pl.multiple_of(c * CH, 8), CH), :]

    def right(c):
        return pltpu.make_async_remote_copy(
            src_ref=chunk(SR, c), dst_ref=chunk(FL, c), send_sem=sr_sem.at[c], recv_sem=fl_sem.at[c],
            device_id=(lax.rem(lev + 1, 4), me), device_id_type=MESH)

    def left(c):
        return pltpu.make_async_remote_copy(
            src_ref=chunk(SL, c), dst_ref=chunk(FR, c), send_sem=sl_sem.at[c], recv_sem=fr_sem.at[c],
            device_id=(lax.rem(lev + 3, 4), me), device_id_type=MESH)

    def each(c, body):
        bg = c // NJ
        j0 = lax.rem(c, NJ) * JC
        for jj in range(JC):
            j = j0 + jj
            rv = PV[pl.ds(bg * 8 * ROWS + j, 8, stride=ROWS), :]

            def at(val, jj=jj):
                return pl.ds(pl.multiple_of(c * CH + (val * JC + jj) * 8, 8), 8)

            def zat(k, j=j):
                return pl.ds(pl.multiple_of((k * ROWS + j) * SEG + bg * 8, 8), 8)

            def put(vals, rv=rv, j=j):
                gv = gain_sq(rv)
                for k in range(LEV):
                    X[pl.ds(bg * 8 * LINES + k * ROWS + j, 8, stride=LINES), :] = vals[k] * gv
            body(rv, at, zat, put)

    def ahead(rv, xs, u, d):
        us = []
        for x in xs:
            d = x if d is None else rv * d + x
            u = d if u is None else rv * u + d
            us.append(u)
        return us, u, d

    def back(rv, us, v, w):
        vs = [None] * LEV
        for k in range(LEV - 1, -1, -1):
            w = us[k] if w is None else rv * w + us[k]
            v = w if v is None else rv * v + w
            vs[k] = v
        return vs, v, w

    def four(q):
        return (1.0 + q * (1.0 + q * (1.0 + q)),
                1.0 + q * (2.0 + q * (3.0 + 4.0 * q)),
                1.0 + q * (4.0 + q * (9.0 + 16.0 * q)))

    def send_out(c):
        @pl.when(lax.rem(c, NJ) == NJ - 1)
        def _():
            loop(8, lambda b: out_copy((c // NJ) * 8 + b).start())

    @pl.when(lev == 0)
    def _():
        def first(c):
            def body(rv, at, zat, put):
                us, u, d = ahead(rv, [Z[zat(k), :] for k in range(LEV)], None, None)
                for k in range(LEV):
                    Z[zat(k), :] = us[k]
                SR[at(0), :] = u
                SR[at(1), :] = d
            each(c, body)
            right(c).start()
        loop(NCH, first)

        def second(c):
            left(c).wait_recv()

            def body(rv, at, zat, put):
                vs, _, _ = back(rv, [Z[zat(k), :] for k in range(LEV)], FR[at(0), :], FR[at(1), :])
                put(vs)
            each(c, body)
            send_out(c)
        loop(NCH, second)
        loop(NCH, lambda c: right(c).wait_send())

    @pl.when(lev == 3)
    def _():
        def first(c):
            def body(rv, at, zat, put):
                us, _, _ = ahead(rv, [Z[zat(k), :] for k in range(LEV)], None, None)
                _, v, w = back(rv, us, None, None)
                SL[at(0), :] = v
                SL[at(1), :] = w
            each(c, body)
            left(c).start()
        loop(NCH, first)

        def second(c):
            right(c).wait_recv()

            def body(rv, at, zat, put):
                us, _, _ = ahead(rv, [Z[zat(k), :] for k in range(LEV)], FL[at(0), :], FL[at(1), :])
                vs, _, _ = back(rv, us, None, None)
                put(vs)
            each(c, body)
            send_out(c)
        loop(NCH, second)
        loop(NCH, lambda c: left(c).wait_send())

    def staged(first, second):
        def step(i):
            @pl.when(i < NCH)
            def _():
                first(i)

            @pl.when(i >= LAG)
            def _():
                second(i - LAG)
        loop(NCH + LAG, step)
        loop(NCH, lambda c: right(c).wait_send())
        loop(NCH, lambda c: left(c).wait_send())

    @pl.when(lev == 1)
    def _():
        def first(c):
            right(c).wait_recv()

            def body(rv, at, zat, put):
                us, u, d = ahead(rv, [Z[zat(k), :] for k in range(LEV)], FL[at(0), :], FL[at(1), :])
                for k in range(LEV):
                    Z[zat(k), :] = us[k]
                SR[at(0), :] = u
                SR[at(1), :] = d
            each(c, body)
            right(c).start()

        def second(c):
            left(c).wait_recv()

            def body(rv, at, zat, put):
                q = rv * rv
                q2 = q * q
                e0, e1, e2 = sums_double(q, 4.0, q2 * q2, *four(q))
                u, d = SR[at(0), :], SR[at(1), :]
                v = FR[at(0), :] + rv * (e1 * u + e2 * d)
                w = FR[at(1), :] + rv * (e0 * u + e1 * d)
                vs, v, w = back(rv, [Z[zat(k), :] for k in range(LEV)], v, w)
                SL[at(0), :] = v
                SL[at(1), :] = w
                put(vs)
            each(c, body)
            left(c).start()
            send_out(c)
        staged(first, second)

    @pl.when(lev == 2)
    def _():
        def first(c):
            left(c).wait_recv()

            def body(rv, at, zat, put):
                us, u, d = ahead(rv, [Z[zat(k), :] for k in range(LEV)], None, None)
                e0, e1, e2 = four(rv * rv)
                v = FR[at(0), :] + rv * (e1 * u + e2 * d)
                w = FR[at(1), :] + rv * (e0 * u + e1 * d)
                _, v, w = back(rv, us, v, w)
                SL[at(0), :] = v
                SL[at(1), :] = w
            each(c, body)
            left(c).start()

        def second(c):
            right(c).wait_recv()

            def body(rv, at, zat, put):
                us, u, d = ahead(rv, [Z[zat(k), :] for k in range(LEV)], FL[at(0), :], FL[at(1), :])
                SR[at(0), :] = u
                SR[at(1), :] = d
                e0, e1, e2 = four(rv * rv)
                v = FR[at(0), :] + rv * (e1 * u + e2 * d)
                w = FR[at(1), :] + rv * (e0 * u + e1 * d)
                vs, _, _ = back(rv, us, v, w)
                put(vs)
            each(c, body)
            right(c).start()
            send_out(c)
        staged(first, second)

    loop(SEG, lambda b: out_copy(b).wait())
    sent(SB, RB, s1_sem, r1_sem)
    sent(RP, CB, s2_sem, r2_sem)


def per_device(control, decay_lon, decay_lat, decay_vert):
    lines = control.reshape(LINES, SEG * LANES)
    lon = jnp.concatenate([decay_lon, decay_lon, decay_lon[:32]])
    lon = jnp.broadcast_to(lon[None, :], (8, LANES))
    lat = jnp.concatenate([decay_lat.reshape(SEG, LANES), jnp.full((8, LANES), 0.5, jnp.float32)])
    any_space = pl.BlockSpec(memory_space=pl.ANY)
    vmem = pl.BlockSpec(memory_space=pltpu.VMEM)
    f32 = jnp.float32
    dma = pltpu.SemaphoreType.DMA
    filtered = pl.pallas_call(
        kernel,
        out_shape=jax.ShapeDtypeStruct((LINES, SEG * LANES), f32),
        in_specs=[any_space, vmem, vmem, any_space],
        out_specs=any_space,
        scratch_shapes=[
            pltpu.VMEM((SEG * LINES + 32, LANES), f32),
            pltpu.VMEM((2 * LANES * SEG, LANES), f32),
            pltpu.VMEM((LINES * SEG, LANES), f32),
            pltpu.VMEM((SEG * ROWS, LANES), f32),
        ] + [pltpu.VMEM((2 * SEG, LANES), f32)] * 4
        + [pltpu.VMEM((NR * MSG, LANES), f32)] * 4
        + [pltpu.VMEM((NCH * CH, LANES), f32)] * 4
        + [dma((SEG,))] * 3 + [dma((NR,))] * 4 + [dma((NCH,))] * 4,
        compiler_params=pltpu.CompilerParams(
            collective_id=0, has_side_effects=True, vmem_limit_bytes=48 * 1024 * 1024),
        name="filters",
    )(lines, lon, lat, decay_vert)
    return filtered.reshape(LEV, ROWS, SEG * LANES)


def solution(mesh):
    in_specs = (P("lev", "row", None), P("row"), P(), P("row", None))
    out_specs = P("lev", "row", None)
    return jax.shard_map(
        per_device, mesh=mesh, in_specs=in_specs, out_specs=out_specs, check_vma=False
    )
```

time: 681 us -> 78.2 us (0.11)
  the two profiles are of different devices: /device:TPU:1 before, /device:TPU:0 now
where the time goes in v1:
time: 78.2 us; the launch traced here: 78 us
  Pallas kernels  72.3 us (92%)
  local copies, waits for them, and re-layouts  4.85 us (6%)
  other arithmetic  0.84 us (1%)
    pallas_call x1, Pallas kernels, per_device(): pl.pallas_call(kernel, out_shape=jax.ShapeDtypeStruct((LINES, SEG * LANES...  72.3 us
    unnamed x5, local copies, waits for them, and re-layouts  4.14 us

profile of v1, /device:TPU:0, one launch (start us, length us, event | category | flops | bytes accessed | tf_op | source)
XLA Modules:
  0.0 78.0 jit_solution(8461246223131392032)
XLA Ops:
  0.0 0.8 %pad_maximum_fusion = f32[128]{0:T(128)S(1)} fusion(f32[32]{0:T(128)} %bitcast.7, f32[48]{0:T(128)} %param.5), kind=kLoop, calls=%fused_computation | loop fusion | flops 256 | bytes 832 | tf_op jit(solution)/shard_map/concatenate | solution.py:524
  0.8 0.7 concatenate.7.dlat
  1.6 0.0 copy-start
  1.6 1.7 %copy-done = f32[4,48,3072]{2,1,0:T(8,128)S(1)} copy-done((f32[4,48,3072]{2,1,0:T(8,128)S(1)}, f32[4,48,3072]{2,1,0:T(8,128)}, u32[]{:S(2)}) %copy-start) | copy-done | bytes 2359320
  3.2 0.0 copy-start.1
  3.2 1.1 %copy-done.1 = f32[48,3072]{1,0:T(8,128)S(1)} copy-done((f32[48,3072]{1,0:T(8,128)S(1)}, f32[48,3072]{1,0:T(8,128)}, u32[]{:S(2)}) %copy-start.1) | copy-done | bytes 589848
  4.3 72.3 %filters.1 = f32[192,3072]{1,0:T(8,128)S(1)} custom-call(f32[192,3072]{1,0:T(8,128)S(1)} %bitcast.5, f32[8,128]{1,0:T(8,128)S(1)} %broadcast_in_dim.2.dlon, f32[32,128]{1,0:T(8,128)S(1)} %concatenate.7.dlat, f32[48,3072]{1,0:T(8,128)S(1)} %copy-done.1), custom_call_target="tpu_custom_call" | custom-call | tf_op jit(solution)/shard_map/filters/pallas_call | solution.py:531
  76.6 1.4 %copy.6 = f32[4,48,3072]{2,1,0:T(8,128)} copy(f32[4,48,3072]{2,1,0:T(8,128)S(1)} %bitcast.4) | data formatting | bytes 4718592
  (1 shorter events, 0.0 us)
Async XLA Ops:
  1.6 1.7 %copy-start = (f32[4,48,3072]{2,1,0:T(8,128)S(1)}, f32[4,48,3072]{2,1,0:T(8,128)}, u32[]{:S(2)}) copy-start(f32[4,48,3072]{2,1,0:T(8,128)} %param.4) | copy-start | bytes 7077892
  3.2 1.1 %copy-start.1 = (f32[48,3072]{1,0:T(8,128)S(1)}, f32[48,3072]{1,0:T(8,128)}, u32[]{:S(2)}) copy-start(f32[48,3072]{1,0:T(8,128)} %dvert.1) | copy-start | bytes 1769476

commit v2 on v1

v2 whole, which is shorter than its diff:
```python
import functools

import jax
import jax.numpy as jnp
from jax import lax
from jax.experimental import pallas as pl
from jax.experimental.pallas import tpu as pltpu
from jax.sharding import PartitionSpec as P

MESH = pl.DeviceIdType.MESH

LANES = 128
SEG = 24
ROWS = 48
LEV = 4
LINES = LEV * ROWS
BG = SEG // 8
NR = 32
MSG = 8
JC = 4
NJ = ROWS // JC
NCH = BG * NJ
CH = 2 * JC * 8
LAG = 4


def gain_sq(r):
    q = r * r
    a = (1.0 - r) * (1.0 + r)
    a2 = a * a
    a4 = a2 * a2
    return jnp.sqrt(a4 * a2 * a / (1.0 + q * (9.0 + q * (9.0 + q))))


def sums_double(q, n, qn, s0, s1, s2):
    return (
        s0 + qn * s0,
        s1 + qn * (s1 + n * s0),
        s2 + qn * (s2 + (2.0 * n) * s1 + (n * n) * s0),
    )


def sums(q, base, doublings):
    s0 = jnp.ones_like(q)
    s1 = jnp.ones_like(q)
    s2 = jnp.ones_like(q)
    qn = q
    for t in range(1, base):
        s0 = s0 + qn
        s1 = s1 + (t + 1.0) * qn
        s2 = s2 + ((t + 1.0) * (t + 1.0)) * qn
        qn = qn * q
    n = float(base)
    for _ in range(doublings):
        s0, s1, s2 = sums_double(q, n, qn, s0, s1, s2)
        qn = qn * qn
        n = 2.0 * n
    return s0, s1, s2


def power(r, base, doublings):
    p = r
    for _ in range(base - 1):
        p = p * r
    for _ in range(doublings):
        p = p * p
    return p


def sublanes():
    return lax.broadcasted_iota(jnp.int32, (8, LANES), 0)


def carry_powers(rn):
    one, two, four = rn, rn * rn, (rn * rn) * (rn * rn)

    def by(idx):
        p = jnp.where(idx % 2 == 1, one, 1.0)
        p = p * jnp.where((idx // 2) % 2 == 1, two, 1.0)
        return p * jnp.where(idx // 4 == 1, four, 1.0)
    return one, two, four, four * four, by(sublanes()), by(7 - sublanes())


def block_carries(us, ds, powers, n, rev):
    r1, r2, r4, r8, up, down = powers
    idx = 7 - sublanes() if rev else sublanes()
    along = down if rev else up
    far = (n * idx.astype(jnp.float32))

    def shifted(x, t):
        return jnp.where(idx >= t, pltpu.roll(x, 8 - t if rev else t, 0), 0.0)

    def last(x):
        row = x[0:1, :] if rev else x[7:8, :]
        return jnp.broadcast_to(row, (8, LANES))

    cu = jnp.zeros((8, LANES), jnp.float32)
    cd = cu
    out = [None] * len(us)
    order = range(len(us))
    for i in (reversed(order) if rev else order):
        u, d = us[i], ds[i]
        for t, rt in ((1, r1), (2, r2), (4, r4)):
            su, sd = shifted(u, t), shifted(d, t)
            u = u + rt * (su + (n * t) * sd)
            d = d + rt * sd
        out[i] = (shifted(u, 1) + along * (cu + far * cd), shifted(d, 1) + along * cd)
        cu, cd = r8 * (cu + (8.0 * n) * cd) + last(u), r8 * cd + last(d)
    return out


def kernel(ctrl, dlon, dlat, dvert, out, X, Y, Z, PV, DN, DL,
           SB, RB, RP, CB, SR, SL, FL, FR,
           in_sem, pv_sem, dn_sem, dl_sem, s1_sem, r1_sem, s2_sem, r2_sem,
           sr_sem, sl_sem, fl_sem, fr_sem):
    lev = lax.axis_index("lev")
    me = lax.axis_index("row")
    barrier = pltpu.get_barrier_semaphore()

    def in_copy(b):
        return pltpu.make_async_copy(
            ctrl.at[:, pl.ds(pl.multiple_of(b * LANES, LANES), LANES)],
            X.at[pl.ds(pl.multiple_of(b * LINES, 8), LINES), :], in_sem.at[b])

    def pv_copy(b):
        return pltpu.make_async_copy(
            dvert.at[:, pl.ds(pl.multiple_of(b * LANES, LANES), LANES)],
            PV.at[pl.ds(pl.multiple_of(b * ROWS, 8), ROWS), :], pv_sem.at[b])

    dn_copy = pltpu.make_async_copy(dlon, DN, dn_sem)
    dl_copy = pltpu.make_async_copy(dlat, DL, dl_sem)

    def loop(n, body, unroll=1):
        def step(i, carry):
            body(i)
            return carry
        lax.fori_loop(0, n, step, 0, unroll=unroll)

    dn_copy.start()
    loop(SEG, lambda b: in_copy(b).start())
    dl_copy.start()
    loop(SEG, lambda b: pv_copy(b).start())

    def greet(i):
        pl.semaphore_signal(barrier, inc=1, device_id=(lev, lax.rem(me + i + 1, NR)), device_id_type=MESH)
    loop(NR - 1, greet)

    @pl.when(lev > 0)
    def _():
        pl.semaphore_signal(barrier, inc=1, device_id=(lev - 1, me), device_id_type=MESH)

    @pl.when(lev < 3)
    def _():
        pl.semaphore_signal(barrier, inc=1, device_id=(lev + 1, me), device_id_type=MESH)

    zero = jnp.zeros((8, LANES), jnp.float32)
    one = jnp.ones((8, LANES), jnp.float32)
    rest = jnp.zeros((LANES - 96, LANES), jnp.float32)
    loop(BG * NR, lambda i: SB.__setitem__((pl.ds(pl.multiple_of(i * MSG, 8), 8), slice(None)), zero))

    def turn_in(i):
        for k in range(4):
            in_copy(4 * i + k).wait()
        for k in range(4):
            b = 4 * i + k
            for g in range(2):
                tile = X[pl.ds(pl.multiple_of(b * LINES + g * 96, 8), 96), :]
                Y[pl.ds(g * LANES * SEG + b, LANES, stride=SEG), :] = jnp.concatenate([tile, rest]).T
    loop(SEG // 4, turn_in)

    dn_copy.wait()
    line = DN[...]
    line = jnp.concatenate([line, line, line[:, :32]], axis=1)
    r = jnp.broadcast_to(line, (8, LANES))
    chains = [(g, bg) for g in range(2) for bg in range(BG)]
    BLK = 4

    def at_lon(g, bg, l):
        return pl.ds(pl.multiple_of((g * LANES + l) * SEG + bg * 8, 8), 8)

    def lon_ends(l, state):
        p, pp, rest = state
        new = []
        for i, (g, bg) in enumerate(chains):
            u, d, v, w = rest[i]
            d = r * d + Y[at_lon(g, bg, l), :]
            u = r * u + d
            new.append((u, d, v + pp * u, w + p * u))
        p = r * p
        return (p, r * pp + p, tuple(new))

    init = (one, one, tuple((zero, zero, zero, zero) for _ in chains))
    _, _, ends = lax.fori_loop(0, LANES, lon_ends, init, unroll=4)

    s0, s1, s2 = sums(r * r, 1, 7)
    lon_powers = carry_powers(power(r, 1, 7))
    n = float(LANES)
    ahead_in, back_in = {}, {}
    for g in range(2):
        of = [ends[g * BG + bg] for bg in range(BG)]
        states = block_carries([e[0] for e in of], [e[1] for e in of], lon_powers, n, False)
        vs = [e[2] + r * (s1 * u + s2 * d) for e, (u, d) in zip(of, states)]
        ws = [e[3] + r * (s0 * u + s1 * d) for e, (u, d) in zip(of, states)]
        backs = block_carries(vs, ws, lon_powers, n, True)
        for bg in range(BG):
            ahead_in[g, bg] = states[bg]
            back_in[g, bg] = backs[bg]

    def lon_ahead(i, state):
        l0 = i * BLK
        xs = [[Y[at_lon(g, bg, l0 + q), :] for g, bg in chains] for q in range(BLK)]
        state = list(state)
        for q in range(BLK):
            for k in range(len(chains)):
                u, d = state[k]
                d = r * d + xs[q][k]
                u = r * u + d
                state[k] = (u, d)
                xs[q][k] = u
        for q in range(BLK):
            for k, (g, bg) in enumerate(chains):
                Y[at_lon(g, bg, l0 + q), :] = xs[q][k]
        return tuple(state)

    lax.fori_loop(0, LANES // BLK, lon_ahead, tuple(ahead_in[ch] for ch in chains))

    g_lon = gain_sq(r)

    def at_lat(k, j, bg):
        return pl.ds(pl.multiple_of((k * ROWS + j) * SEG + bg * 8, 8), 8)

    def slot(ref, bg, i):
        return ref.at[pl.ds(pl.multiple_of((bg * NR + i) * MSG, 8), MSG), :]

    def message(src, dst, ssem, rsem, bg, p, at):
        return pltpu.make_async_remote_copy(
            src_ref=slot(src, bg, p), dst_ref=slot(dst, bg, at), send_sem=ssem.at[bg * NR + p],
            recv_sem=rsem.at[bg * NR + at], device_id=(lev, p), device_id_type=MESH)

    def send(src, dst, ssem, rsem, bg):
        def to(i):
            p = lax.rem(me + i + 1, NR)
            message(src, dst, ssem, rsem, bg, p, me).start()
        loop(NR - 1, to)
        at = pl.ds(pl.multiple_of((bg * NR + me) * MSG, 8), MSG)
        dst[at, :] = src[at, :]

    def get(src, dst, ssem, rsem, bg):
        def of(i):
            p = lax.rem(me + i + 1, NR)
            message(src, dst, ssem, rsem, bg, p, p).wait_recv()
        loop(NR - 1, of)

    def sent(src, dst, ssem, rsem, bg):
        def to(i):
            p = lax.rem(me + i + 1, NR)
            message(src, dst, ssem, rsem, bg, p, me).wait_send()
        loop(NR - 1, to)

    for bg in range(BG):
        def lon_back(i, state, bg=bg):
            l0 = LANES - BLK - i * BLK
            xs = [[Y[at_lon(g, bg, l0 + q), :] for g in range(2)] for q in range(BLK)]
            state = list(state)
            for q in range(BLK - 1, -1, -1):
                for g in range(2):
                    v, w = state[g]
                    w = r * w + xs[q][g]
                    v = r * v + w
                    state[g] = (v, w)
                    xs[q][g] = v * g_lon
            for q in range(BLK):
                for g in range(2):
                    Y[at_lon(g, bg, l0 + q), :] = xs[q][g]
            return tuple(state)

        lax.fori_loop(0, LANES // BLK, lon_back, (back_in[0, bg], back_in[1, bg]), unroll=2)

        def turn_out(i, bg=bg):
            for q in range(4):
                b = bg * 8 + i * 4 + q
                for g in range(2):
                    tile = Y[pl.ds(g * LANES * SEG + b, LANES, stride=SEG), :].T
                    for k in range(2):
                        Z[pl.ds((2 * g + k) * ROWS * SEG + b, ROWS, stride=SEG), :] = tile[k * ROWS:(k + 1) * ROWS, :]
        loop(2, turn_out)

        if bg == 0:
            dl_copy.wait()
        rl = DL[bg * 8:(bg + 1) * 8, :]

        def lat_ends(j, state, rl=rl, bg=bg):
            p, pp, rest = state
            new = []
            for k in range(LEV):
                u, d, v, w = rest[k]
                d = rl * d + Z[at_lat(k, j, bg), :]
                u = rl * u + d
                new.append((u, d, v + pp * u, w + p * u))
            p = rl * p
            return (p, rl * pp + p, tuple(new))

        init = (one, one, tuple((zero, zero, zero, zero) for _ in range(LEV)))
        _, _, ends = lax.fori_loop(0, ROWS, lat_ends, init, unroll=4)
        for k in range(LEV):
            for val in range(4):
                SB[pl.ds((bg * NR + k * 8) * MSG + val, 8, stride=MSG), :] = ends[k][val]
        if bg == 0:
            neighbours = (lev > 0).astype(jnp.int32) + (lev < 3).astype(jnp.int32)
            pl.semaphore_wait(barrier, NR - 1 + neighbours)
        send(SB, RB, s1_sem, r1_sem, bg)

    m = float(ROWS)
    for bg in range(BG):
        ro = jnp.broadcast_to(DL[pl.ds(bg * 8 + lax.rem(me, 8), 1), :], (8, LANES))
        o0, o1, o2 = sums(ro * ro, 3, 4)
        own_powers = carry_powers(power(ro, 3, 4))
        get(SB, RB, s1_sem, r1_sem, bg)

        def rows_of(q, val, bg=bg):
            return pl.ds((bg * NR + q * 8) * MSG + val, 8, stride=MSG)

        def had(val):
            return [RB[rows_of(q, val), :] for q in range(NR // 8)]
        states = block_carries(had(0), had(1), own_powers, m, False)
        vs = [e + ro * (o1 * u + o2 * d) for e, (u, d) in zip(had(2), states)]
        ws = [e + ro * (o0 * u + o1 * d) for e, (u, d) in zip(had(3), states)]
        backs = block_carries(vs, ws, own_powers, m, True)
        for q in range(NR // 8):
            RP[rows_of(q, 0), :], RP[rows_of(q, 1), :] = states[q]
            RP[rows_of(q, 2), :], RP[rows_of(q, 3), :] = backs[q]
            for val in range(4, MSG):
                RP[rows_of(q, val), :] = zero
        send(RP, CB, s2_sem, r2_sem, bg)

    def lat_finish(bg):
        get(RP, CB, s2_sem, r2_sem, bg)
        rl = DL[pl.ds(pl.multiple_of(bg * 8, 8), 8), :]
        g_lat = gain_sq(rl)

        def come(k, val):
            return CB[pl.ds((bg * NR + k * 8) * MSG + val, 8, stride=MSG), :]

        def lat_ahead(i, state):
            xs = [[Z[at_lat(k, i * BLK + q, bg), :] for k in range(LEV)] for q in range(BLK)]
            state = list(state)
            for q in range(BLK):
                for k in range(LEV):
                    u, d = state[k]
                    d = rl * d + xs[q][k]
                    u = rl * u + d
                    state[k] = (u, d)
                    xs[q][k] = u
            for q in range(BLK):
                for k in range(LEV):
                    Z[at_lat(k, i * BLK + q, bg), :] = xs[q][k]
            return tuple(state)
        lax.fori_loop(0, ROWS // BLK, lat_ahead, tuple((come(k, 0), come(k, 1)) for k in range(LEV)))

        def lat_back(i, state):
            j0 = ROWS - BLK - i * BLK
            xs = [[Z[at_lat(k, j0 + q, bg), :] for k in range(LEV)] for q in range(BLK)]
            state = list(state)
            for q in range(BLK - 1, -1, -1):
                for k in range(LEV):
                    v, w = state[k]
                    w = rl * w + xs[q][k]
                    v = rl * v + w
                    state[k] = (v, w)
                    xs[q][k] = v * g_lat
            for q in range(BLK):
                for k in range(LEV):
                    Z[at_lat(k, j0 + q, bg), :] = xs[q][k]
            return tuple(state)
        lax.fori_loop(0, ROWS // BLK, lat_back, tuple((come(k, 2), come(k, 3)) for k in range(LEV)))

    loop(SEG, lambda b: pv_copy(b).wait())

    def chunk(ref, c):
        return ref.at[pl.ds(pl.multiple_of(c * CH, 8), CH), :]

    def right(c):
        return pltpu.make_async_remote_copy(
            src_ref=chunk(SR, c), dst_ref=chunk(FL, c), send_sem=sr_sem.at[c], recv_sem=fl_sem.at[c],
            device_id=(lax.rem(lev + 1, 4), me), device_id_type=MESH)

    def left(c):
        return pltpu.make_async_remote_copy(
            src_ref=chunk(SL, c), dst_ref=chunk(FR, c), send_sem=sl_sem.at[c], recv_sem=fr_sem.at[c],
            device_id=(lax.rem(lev + 3, 4), me), device_id_type=MESH)

    def each(c, body):
        bg = c // NJ
        j0 = lax.rem(c, NJ) * JC
        for jj in range(JC):
            j = j0 + jj
            rv = PV[pl.ds(bg * 8 * ROWS + j, 8, stride=ROWS), :]

            def at(val, jj=jj):
                return pl.ds(pl.multiple_of(c * CH + (val * JC + jj) * 8, 8), 8)

            def zat(k, j=j):
                return pl.ds(pl.multiple_of((k * ROWS + j) * SEG + bg * 8, 8), 8)

            def put(vals, rv=rv, j=j):
                gv = gain_sq(rv)
                for k in range(LEV):
                    X[pl.ds(bg * 8 * LINES + k * ROWS + j, 8, stride=LINES), :] = vals[k] * gv
            body(rv, at, zat, put)

    def ahead(rv, xs, u, d):
        us = []
        for x in xs:
            d = x if d is None else rv * d + x
            u = d if u is None else rv * u + d
            us.append(u)
        return us, u, d

    def back(rv, us, v, w):
        vs = [None] * LEV
        for k in range(LEV - 1, -1, -1):
            w = us[k] if w is None else rv * w + us[k]
            v = w if v is None else rv * v + w
            vs[k] = v
        return vs, v, w

    def four(q):
        return (1.0 + q * (1.0 + q * (1.0 + q)),
                1.0 + q * (2.0 + q * (3.0 + 4.0 * q)),
                1.0 + q * (4.0 + q * (9.0 + 16.0 * q)))

    def send_out(c):
        @pl.when(lax.rem(c, 2) == 1)
        def _():
            bg = c // NJ
            j0 = lax.rem(c - 1, NJ) * JC
            for k in range(LEV):
                for b in range(8):
                    at = pl.ds(pl.multiple_of((bg * 8 + b) * LINES + k * ROWS + j0, 8), 8)
                    out[pl.ds(pl.multiple_of(k * ROWS + j0, 8), 8),
                        pl.ds(pl.multiple_of((bg * 8 + b) * LANES, LANES), LANES)] = X[at, :]

    def ready(c):
        @pl.when(lax.rem(c, NJ) == 0)
        def _():
            lat_finish(c // NJ)

    @pl.when(lev == 0)
    def _():
        def first(c):
            ready(c)

            def body(rv, at, zat, put):
                us, u, d = ahead(rv, [Z[zat(k), :] for k in range(LEV)], None, None)
                for k in range(LEV):
                    Z[zat(k), :] = us[k]
                SR[at(0), :] = u
                SR[at(1), :] = d
            each(c, body)
            right(c).start()
        loop(NCH, first)

        def second(c):
            left(c).wait_recv()

            def body(rv, at, zat, put):
                vs, _, _ = back(rv, [Z[zat(k), :] for k in range(LEV)], FR[at(0), :], FR[at(1), :])
                put(vs)
            each(c, body)
            send_out(c)
        loop(NCH, second)
        loop(NCH, lambda c: right(c).wait_send())

    @pl.when(lev == 3)
    def _():
        def first(c):
            ready(c)

            def body(rv, at, zat, put):
                us, _, _ = ahead(rv, [Z[zat(k), :] for k in range(LEV)], None, None)
                _, v, w = back(rv, us, None, None)
                SL[at(0), :] = v
                SL[at(1), :] = w
            each(c, body)
            left(c).start()
        loop(NCH, first)

        def second(c):
            right(c).wait_recv()

            def body(rv, at, zat, put):
                us, _, _ = ahead(rv, [Z[zat(k), :] for k in range(LEV)], FL[at(0), :], FL[at(1), :])
                vs, _, _ = back(rv, us, None, None)
                put(vs)
            each(c, body)
            send_out(c)
        loop(NCH, second)
        loop(NCH, lambda c: left(c).wait_send())

    def staged(first, second):
        def step(i):
            @pl.when(i < NCH)
            def _():
                first(i)

            @pl.when(i >= LAG)
            def _():
                second(i - LAG)
        loop(NCH + LAG, step)
        loop(NCH, lambda c: right(c).wait_send())
        loop(NCH, lambda c: left(c).wait_send())

    @pl.when(lev == 1)
    def _():
        def first(c):
            ready(c)

            right(c).wait_recv()

            def body(rv, at, zat, put):
                us, u, d = ahead(rv, [Z[zat(k), :] for k in range(LEV)], FL[at(0), :], FL[at(1), :])
                for k in range(LEV):
                    Z[zat(k), :] = us[k]
                SR[at(0), :] = u
                SR[at(1), :] = d
            each(c, body)
            right(c).start()

        def second(c):
            left(c).wait_recv()

            def body(rv, at, zat, put):
                q = rv * rv
                q2 = q * q
                e0, e1, e2 = sums_double(q, 4.0, q2 * q2, *four(q))
                u, d = SR[at(0), :], SR[at(1), :]
                v = FR[at(0), :] + rv * (e1 * u + e2 * d)
                w = FR[at(1), :] + rv * (e0 * u + e1 * d)
                vs, v, w = back(rv, [Z[zat(k), :] for k in range(LEV)], v, w)
                SL[at(0), :] = v
                SL[at(1), :] = w
                put(vs)
            each(c, body)
            left(c).start()
            send_out(c)
        staged(first, second)

    @pl.when(lev == 2)
    def _():
        def first(c):
            ready(c)

            left(c).wait_recv()

            def body(rv, at, zat, put):
                us, u, d = ahead(rv, [Z[zat(k), :] for k in range(LEV)], None, None)
                e0, e1, e2 = four(rv * rv)
                v = FR[at(0), :] + rv * (e1 * u + e2 * d)
                w = FR[at(1), :] + rv * (e0 * u + e1 * d)
                _, v, w = back(rv, us, v, w)
                SL[at(0), :] = v
                SL[at(1), :] = w
            each(c, body)
            left(c).start()

        def second(c):
            right(c).wait_recv()

            def body(rv, at, zat, put):
                us, u, d = ahead(rv, [Z[zat(k), :] for k in range(LEV)], FL[at(0), :], FL[at(1), :])
                SR[at(0), :] = u
                SR[at(1), :] = d
                e0, e1, e2 = four(rv * rv)
                v = FR[at(0), :] + rv * (e1 * u + e2 * d)
                w = FR[at(1), :] + rv * (e0 * u + e1 * d)
                vs, _, _ = back(rv, us, v, w)
                put(vs)
            each(c, body)
            right(c).start()
            send_out(c)
        staged(first, second)

    for bg in range(BG):
        sent(SB, RB, s1_sem, r1_sem, bg)
        sent(RP, CB, s2_sem, r2_sem, bg)


def per_device(control, decay_lon, decay_lat, decay_vert):
    lines = control.reshape(LINES, SEG * LANES)
    hbm = pl.BlockSpec(memory_space=pltpu.HBM)
    vmem = pl.BlockSpec(memory_space=pltpu.VMEM)
    f32 = jnp.float32
    dma = pltpu.SemaphoreType.DMA
    filtered = pl.pallas_call(
        kernel,
        out_shape=jax.ShapeDtypeStruct((LINES, SEG * LANES), f32),
        in_specs=[hbm] * 4,
        out_specs=vmem,
        scratch_shapes=[
            pltpu.VMEM((SEG * LINES, LANES), f32),
            pltpu.VMEM((2 * LANES * SEG, LANES), f32),
            pltpu.VMEM((LINES * SEG, LANES), f32),
            pltpu.VMEM((SEG * ROWS, LANES), f32),
            pltpu.VMEM((1, ROWS), f32),
            pltpu.VMEM((SEG, LANES), f32),
        ] + [pltpu.VMEM((BG * NR * MSG, LANES), f32)] * 4
        + [pltpu.VMEM((NCH * CH, LANES), f32)] * 4
        + [dma((SEG,))] * 2 + [dma] * 2 + [dma((BG * NR,))] * 4 + [dma((NCH,))] * 4,
        compiler_params=pltpu.CompilerParams(
            collective_id=0, has_side_effects=True, vmem_limit_bytes=48 * 1024 * 1024),
        name="filters",
    )(lines, decay_lon.reshape(1, ROWS), decay_lat.reshape(SEG, LANES), decay_vert)
    return filtered.reshape(LEV, ROWS, SEG * LANES)


def solution(mesh):
    in_specs = (P("lev", "row", None), P("row"), P(), P("row", None))
    out_specs = P("lev", "row", None)
    return jax.shard_map(
        per_device, mesh=mesh, in_specs=in_specs, out_specs=out_specs, check_vma=False
    )
```

time: 78.2 us -> 70.3 us (0.90)
  Pallas kernels: 72.3 us -> 64.5 us
  other arithmetic: 0.84 us -> 0 us
    pallas_call x1, Pallas kernels: 72.3 us -> 64.5 us  [per_device(): pl.pallas_call(kernel, out_shape=jax.ShapeDtypeStruct((LINES, SEG * LANES...]
    unnamed x5 -> x9, local copies, waits for them, and re-layouts: 4.14 us -> 5.5 us
    concatenate x1 -> x0, other arithmetic: 0.84 us -> none  [per_device(): lon = jnp.concatenate([decay_lon, decay_lon, decay_lon[:32]])]
where the time goes in v2:
time: 70.3 us; the launch traced here: 70.1 us
  Pallas kernels  64.5 us (92%)
  local copies, waits for them, and re-layouts  5.5 us (8%)
    pallas_call x1, Pallas kernels, per_device(): pl.pallas_call(kernel, out_shape=jax.ShapeDtypeStruct((LINES, SEG * LANES...  64.5 us
    unnamed x9, local copies, waits for them, and re-layouts  5.5 us

profile of v2, /device:TPU:0, one launch (start us, length us, event | category | flops | bytes accessed | tf_op | source)
XLA Modules:
  0.0 70.1 jit_solution(1237035037550414797)
XLA Ops:
  0.0 0.0 copy-start
  0.0 1.7 %copy-done = f32[4,48,3072]{2,1,0:T(8,128)S(1)} copy-done((f32[4,48,3072]{2,1,0:T(8,128)S(1)}, f32[4,48,3072]{2,1,0:T(8,128)}, u32[]{:S(2)}) %copy-start) | copy-done | bytes 2359320
  1.7 0.0 copy-start.1
  1.7 1.1 %copy-done.1 = f32[48,3072]{1,0:T(8,128)S(1)} copy-done((f32[48,3072]{1,0:T(8,128)S(1)}, f32[48,3072]{1,0:T(8,128)}, u32[]{:S(2)}) %copy-start.1) | copy-done | bytes 589848
  2.7 0.0 copy-start.2
  2.7 0.7 %copy-done.2 = f32[3072]{0:T(1024)S(1)} copy-done((f32[3072]{0:T(1024)S(1)}, f32[3072]{0:T(1024)}, u32[]{:S(2)}) %copy-start.2) | copy-done | bytes 12312
  3.4 0.0 copy-start.3
  3.4 0.7 copy-done.3
  4.1 64.5 %filters.1 = f32[192,3072]{1,0:T(8,128)S(1)} custom-call(f32[192,3072]{1,0:T(8,128)S(1)} %bitcast.5, f32[1,48]{1,0:T(1,128)S(1)} %bitcast.7, f32[24,128]{1,0:T(8,128)S(1)} %bitcast.6, f32[48,3072]{1,0:T(8,128)S(1)} %copy-done.1), custom_call_target="tpu_custom_call" | custom-call | tf_op jit(solution)/shard_map/filters/pallas_call | solution.py:594
  68.6 1.4 %copy.6 = f32[4,48,3072]{2,1,0:T(8,128)} copy(f32[4,48,3072]{2,1,0:T(8,128)S(1)} %bitcast.4) | data formatting | bytes 4718592
Async XLA Ops:
  0.0 1.7 %copy-start = (f32[4,48,3072]{2,1,0:T(8,128)S(1)}, f32[4,48,3072]{2,1,0:T(8,128)}, u32[]{:S(2)}) copy-start(f32[4,48,3072]{2,1,0:T(8,128)} %param.4) | copy-start | bytes 7077892
  1.7 1.1 %copy-start.1 = (f32[48,3072]{1,0:T(8,128)S(1)}, f32[48,3072]{1,0:T(8,128)}, u32[]{:S(2)}) copy-start(f32[48,3072]{1,0:T(8,128)} %dvert.1) | copy-start | bytes 1769476
  2.7 0.7 %copy-start.2 = (f32[3072]{0:T(1024)S(1)}, f32[3072]{0:T(1024)}, u32[]{:S(2)}) copy-start(f32[3072]{0:T(1024)} %param.6) | copy-start | bytes 36868
  3.4 0.7 copy-start.3

commit v3 on v2

--- a/solution.py
+++ b/solution.py
@@ -21,7 +21,7 @@
 NJ = ROWS // JC
 NCH = BG * NJ
 CH = 2 * JC * 8
-LAG = 4
+LAG = 6
 
 
 def gain_sq(r):
@@ -607,9 +607,9 @@
         + [pltpu.VMEM((NCH * CH, LANES), f32)] * 4
         + [dma((SEG,))] * 2 + [dma] * 2 + [dma((BG * NR,))] * 4 + [dma((NCH,))] * 4,
         compiler_params=pltpu.CompilerParams(
-            collective_id=0, has_side_effects=True, vmem_limit_bytes=48 * 1024 * 1024),
+            collective_id=0, has_side_effects=True, vmem_limit_bytes=50 * 1024 * 1024),
         name="filters",
-    )(lines, decay_lon.reshape(1, ROWS), decay_lat.reshape(SEG, LANES), decay_vert)
+    )(*[pltpu.with_memory_space_constraint(x, pltpu.HBM) for x in (lines, decay_lon.reshape(1, ROWS), decay_lat.reshape(SEG, LANES), decay_vert)])
     return filtered.reshape(LEV, ROWS, SEG * LANES)
 
 

time: 70.3 us -> 64.5 us (0.917)
  local copies, waits for them, and re-layouts: 5.5 us -> 1.41 us
  Pallas kernels: 64.5 us -> 63 us
    unnamed x9 -> x1, local copies, waits for them, and re-layouts: 5.5 us -> 1.41 us
    pallas_call x1, Pallas kernels: 64.5 us -> 63 us  [per_device(): pl.pallas_call(kernel, out_shape=jax.ShapeDtypeStruct((LINES, SEG * LANES...]
where the time goes in v3:
time: 64.5 us; the launch traced here: 64.4 us
  Pallas kernels  63 us (98%)
  local copies, waits for them, and re-layouts  1.41 us (2%)
    pallas_call x1, Pallas kernels, per_device(): pl.pallas_call(kernel, out_shape=jax.ShapeDtypeStruct((LINES, SEG * LANES...  63 us
    unnamed x1, local copies, waits for them, and re-layouts  1.41 us

profile of v3, /device:TPU:0, one launch (start us, length us, event | category | flops | bytes accessed | tf_op | source)
XLA Modules:
  0.0 64.4 jit_solution(2957990181877564787)
XLA Ops:
  0.0 63.0 %filters.1 = f32[192,3072]{1,0:T(8,128)S(1)} custom-call(f32[192,3072]{1,0:T(8,128)} %bitcast.5, f32[1,48]{1,0:T(1,128)} %bitcast.7, f32[24,128]{1,0:T(8,128)} %bitcast.6, f32[48,3072]{1,0:T(8,128)} %dvert.1), custom_call_target="tpu_custom_call" | custom-call | tf_op jit(solution)/shard_map/filters/pallas_call | solution.py:594
  63.0 1.4 %copy.6 = f32[4,48,3072]{2,1,0:T(8,128)} copy(f32[4,48,3072]{2,1,0:T(8,128)S(1)} %bitcast.4) | data formatting | bytes 4718592

commit v4 on v3

--- a/solution.py
+++ b/solution.py
@@ -22,6 +22,7 @@
 NCH = BG * NJ
 CH = 2 * JC * 8
 LAG = 6
+IN = 48
 
 
 def gain_sq(r):
@@ -109,7 +110,7 @@
     return out
 
 
-def kernel(ctrl, dlon, dlat, dvert, out, X, Y, Z, PV, DN, DL,
+def kernel(ctrl, dlon, dlat, dvert, out, X, Y, Z, PI, PV, OS, DN, DL,
            SB, RB, RP, CB, SR, SL, FL, FR,
            in_sem, pv_sem, dn_sem, dl_sem, s1_sem, r1_sem, s2_sem, r2_sem,
            sr_sem, sl_sem, fl_sem, fr_sem):
@@ -117,16 +118,11 @@
     me = lax.axis_index("row")
     barrier = pltpu.get_barrier_semaphore()
 
-    def in_copy(b):
-        return pltpu.make_async_copy(
-            ctrl.at[:, pl.ds(pl.multiple_of(b * LANES, LANES), LANES)],
-            X.at[pl.ds(pl.multiple_of(b * LINES, 8), LINES), :], in_sem.at[b])
-
-    def pv_copy(b):
-        return pltpu.make_async_copy(
-            dvert.at[:, pl.ds(pl.multiple_of(b * LANES, LANES), LANES)],
-            PV.at[pl.ds(pl.multiple_of(b * ROWS, 8), ROWS), :], pv_sem.at[b])
-
+    def in_copy(i):
+        at = pl.ds(pl.multiple_of(i * IN, 8), IN)
+        return pltpu.make_async_copy(ctrl.at[at, :], X.at[at, :], in_sem.at[i])
+
+    pv_copy = pltpu.make_async_copy(dvert, PI, pv_sem)
     dn_copy = pltpu.make_async_copy(dlon, DN, dn_sem)
     dl_copy = pltpu.make_async_copy(dlat, DL, dl_sem)
 
@@ -137,9 +133,10 @@
         lax.fori_loop(0, n, step, 0, unroll=unroll)
 
     dn_copy.start()
-    loop(SEG, lambda b: in_copy(b).start())
+    for i in range(LINES // IN):
+        in_copy(i).start()
     dl_copy.start()
-    loop(SEG, lambda b: pv_copy(b).start())
+    pv_copy.start()
 
     def greet(i):
         pl.semaphore_signal(barrier, inc=1, device_id=(lev, lax.rem(me + i + 1, NR)), device_id_type=MESH)
@@ -158,15 +155,16 @@
     rest = jnp.zeros((LANES - 96, LANES), jnp.float32)
     loop(BG * NR, lambda i: SB.__setitem__((pl.ds(pl.multiple_of(i * MSG, 8), 8), slice(None)), zero))
 
-    def turn_in(i):
-        for k in range(4):
-            in_copy(4 * i + k).wait()
-        for k in range(4):
-            b = 4 * i + k
-            for g in range(2):
-                tile = X[pl.ds(pl.multiple_of(b * LINES + g * 96, 8), 96), :]
+    for g in range(2):
+        for i in range(96 // IN):
+            in_copy(g * (96 // IN) + i).wait()
+
+        def turn_in(i, g=g):
+            for k in range(8):
+                b = 8 * i + k
+                tile = X[pl.ds(g * 96, 96), pl.ds(pl.multiple_of(b * LANES, LANES), LANES)]
                 Y[pl.ds(g * LANES * SEG + b, LANES, stride=SEG), :] = jnp.concatenate([tile, rest]).T
-    loop(SEG // 4, turn_in)
+        loop(SEG // 8, turn_in)
 
     dn_copy.wait()
     line = DN[...]
@@ -232,30 +230,21 @@
     def slot(ref, bg, i):
         return ref.at[pl.ds(pl.multiple_of((bg * NR + i) * MSG, 8), MSG), :]
 
-    def message(src, dst, ssem, rsem, bg, p, at):
-        return pltpu.make_async_remote_copy(
-            src_ref=slot(src, bg, p), dst_ref=slot(dst, bg, at), send_sem=ssem.at[bg * NR + p],
-            recv_sem=rsem.at[bg * NR + at], device_id=(lev, p), device_id_type=MESH)
-
     def send(src, dst, ssem, rsem, bg):
         def to(i):
             p = lax.rem(me + i + 1, NR)
-            message(src, dst, ssem, rsem, bg, p, me).start()
+            pltpu.make_async_remote_copy(
+                src_ref=slot(src, bg, p), dst_ref=slot(dst, bg, me), send_sem=ssem.at[bg],
+                recv_sem=rsem.at[bg], device_id=(lev, p), device_id_type=MESH).start()
         loop(NR - 1, to)
         at = pl.ds(pl.multiple_of((bg * NR + me) * MSG, 8), MSG)
         dst[at, :] = src[at, :]
 
-    def get(src, dst, ssem, rsem, bg):
-        def of(i):
-            p = lax.rem(me + i + 1, NR)
-            message(src, dst, ssem, rsem, bg, p, p).wait_recv()
-        loop(NR - 1, of)
-
-    def sent(src, dst, ssem, rsem, bg):
-        def to(i):
-            p = lax.rem(me + i + 1, NR)
-            message(src, dst, ssem, rsem, bg, p, me).wait_send()
-        loop(NR - 1, to)
+    def all_of(src, dst, ssem, rsem, bg):
+        at = pl.ds(pl.multiple_of(bg * NR * MSG, 8), (NR - 1) * MSG)
+        return pltpu.make_async_remote_copy(
+            src_ref=src.at[at, :], dst_ref=dst.at[at, :], send_sem=ssem.at[bg], recv_sem=rsem.at[bg],
+            device_id=(lev, lax.rem(me + 1, NR)), device_id_type=MESH)
 
     for bg in range(BG):
         def lon_back(i, state, bg=bg):
@@ -310,12 +299,20 @@
             pl.semaphore_wait(barrier, NR - 1 + neighbours)
         send(SB, RB, s1_sem, r1_sem, bg)
 
+    pv_copy.wait()
+
+    def place(b):
+        for q in range(ROWS // 8):
+            PV[pl.ds(pl.multiple_of(b * ROWS + q * 8, 8), 8), :] = PI[
+                q * 8:(q + 1) * 8, pl.ds(pl.multiple_of(b * LANES, LANES), LANES)]
+    loop(SEG, place, unroll=2)
+
     m = float(ROWS)
     for bg in range(BG):
         ro = jnp.broadcast_to(DL[pl.ds(bg * 8 + lax.rem(me, 8), 1), :], (8, LANES))
         o0, o1, o2 = sums(ro * ro, 3, 4)
         own_powers = carry_powers(power(ro, 3, 4))
-        get(SB, RB, s1_sem, r1_sem, bg)
+        all_of(SB, RB, s1_sem, r1_sem, bg).wait_recv()
 
         def rows_of(q, val, bg=bg):
             return pl.ds((bg * NR + q * 8) * MSG + val, 8, stride=MSG)
@@ -334,7 +331,7 @@
         send(RP, CB, s2_sem, r2_sem, bg)
 
     def lat_finish(bg):
-        get(RP, CB, s2_sem, r2_sem, bg)
+        all_of(RP, CB, s2_sem, r2_sem, bg).wait_recv()
         rl = DL[pl.ds(pl.multiple_of(bg * 8, 8), 8), :]
         g_lat = gain_sq(rl)
 
@@ -374,19 +371,21 @@
             return tuple(state)
         lax.fori_loop(0, ROWS // BLK, lat_back, tuple((come(k, 2), come(k, 3)) for k in range(LEV)))
 
-    loop(SEG, lambda b: pv_copy(b).wait())
 
     def chunk(ref, c):
-        return ref.at[pl.ds(pl.multiple_of(c * CH, 8), CH), :]
+        return ref if c is None else ref.at[pl.ds(pl.multiple_of(c * CH, 8), CH), :]
+
+    def one_of(sem, c):
+        return sem.at[0 if c is None else c]
 
     def right(c):
         return pltpu.make_async_remote_copy(
-            src_ref=chunk(SR, c), dst_ref=chunk(FL, c), send_sem=sr_sem.at[c], recv_sem=fl_sem.at[c],
+            src_ref=chunk(SR, c), dst_ref=chunk(FL, c), send_sem=sr_sem, recv_sem=one_of(fl_sem, c),
             device_id=(lax.rem(lev + 1, 4), me), device_id_type=MESH)
 
     def left(c):
         return pltpu.make_async_remote_copy(
-            src_ref=chunk(SL, c), dst_ref=chunk(FR, c), send_sem=sl_sem.at[c], recv_sem=fr_sem.at[c],
+            src_ref=chunk(SL, c), dst_ref=chunk(FR, c), send_sem=sl_sem, recv_sem=one_of(fr_sem, c),
             device_id=(lax.rem(lev + 3, 4), me), device_id_type=MESH)
 
     def each(c, body):
@@ -405,7 +404,7 @@
             def put(vals, rv=rv, j=j):
                 gv = gain_sq(rv)
                 for k in range(LEV):
-                    X[pl.ds(bg * 8 * LINES + k * ROWS + j, 8, stride=LINES), :] = vals[k] * gv
+                    OS[pl.ds(k * 8 + lax.rem(j, 8), 8, stride=LEV * 8), :] = vals[k] * gv
             body(rv, at, zat, put)
 
     def ahead(rv, xs, u, d):
@@ -436,9 +435,9 @@
             j0 = lax.rem(c - 1, NJ) * JC
             for k in range(LEV):
                 for b in range(8):
-                    at = pl.ds(pl.multiple_of((bg * 8 + b) * LINES + k * ROWS + j0, 8), 8)
                     out[pl.ds(pl.multiple_of(k * ROWS + j0, 8), 8),
-                        pl.ds(pl.multiple_of((bg * 8 + b) * LANES, LANES), LANES)] = X[at, :]
+                        pl.ds(pl.multiple_of((bg * 8 + b) * LANES, LANES), LANES)] = OS[
+                            (b * LEV + k) * 8:(b * LEV + k + 1) * 8, :]
 
     def ready(c):
         @pl.when(lax.rem(c, NJ) == 0)
@@ -469,7 +468,7 @@
             each(c, body)
             send_out(c)
         loop(NCH, second)
-        loop(NCH, lambda c: right(c).wait_send())
+        right(None).wait_send()
 
     @pl.when(lev == 3)
     def _():
@@ -495,7 +494,7 @@
             each(c, body)
             send_out(c)
         loop(NCH, second)
-        loop(NCH, lambda c: left(c).wait_send())
+        left(None).wait_send()
 
     def staged(first, second):
         def step(i):
@@ -507,8 +506,8 @@
             def _():
                 second(i - LAG)
         loop(NCH + LAG, step)
-        loop(NCH, lambda c: right(c).wait_send())
-        loop(NCH, lambda c: left(c).wait_send())
+        right(None).wait_send()
+        left(None).wait_send()
 
     @pl.when(lev == 1)
     def _():
@@ -581,8 +580,8 @@
         staged(first, second)
 
     for bg in range(BG):
-        sent(SB, RB, s1_sem, r1_sem, bg)
-        sent(RP, CB, s2_sem, r2_sem, bg)
+        all_of(SB, RB, s1_sem, r1_sem, bg).wait_send()
+        all_of(RP, CB, s2_sem, r2_sem, bg).wait_send()
 
 
 def per_device(control, decay_lon, decay_lat, decay_vert):
@@ -597,15 +596,17 @@
         in_specs=[hbm] * 4,
         out_specs=vmem,
         scratch_shapes=[
-            pltpu.VMEM((SEG * LINES, LANES), f32),
+            pltpu.VMEM((LINES, SEG * LANES), f32),
             pltpu.VMEM((2 * LANES * SEG, LANES), f32),
             pltpu.VMEM((LINES * SEG, LANES), f32),
+            pltpu.VMEM((ROWS, SEG * LANES), f32),
             pltpu.VMEM((SEG * ROWS, LANES), f32),
+            pltpu.VMEM((8 * LEV * 8, LANES), f32),
             pltpu.VMEM((1, ROWS), f32),
             pltpu.VMEM((SEG, LANES), f32),
         ] + [pltpu.VMEM((BG * NR * MSG, LANES), f32)] * 4
         + [pltpu.VMEM((NCH * CH, LANES), f32)] * 4
-        + [dma((SEG,))] * 2 + [dma] * 2 + [dma((BG * NR,))] * 4 + [dma((NCH,))] * 4,
+        + [dma((LINES // IN,))] + [dma] * 3 + [dma((BG,))] * 4 + [dma] * 2 + [dma((NCH,))] * 2,
         compiler_params=pltpu.CompilerParams(
             collective_id=0, has_side_effects=True, vmem_limit_bytes=50 * 1024 * 1024),
         name="filters",

time: 64.5 us -> 56.5 us (0.88)
  Pallas kernels: 63 us -> 55 us
    pallas_call x1, Pallas kernels: 63 us -> 55 us  [per_device(): pl.pallas_call(kernel, out_shape=jax.ShapeDtypeStruct((LINES, SEG * LANES...]
where the time goes in v4:
time: 56.5 us; the launch traced here: 56.4 us
  Pallas kernels  55 us (97%)
  local copies, waits for them, and re-layouts  1.41 us (2%)
    pallas_call x1, Pallas kernels, per_device(): pl.pallas_call(kernel, out_shape=jax.ShapeDtypeStruct((LINES, SEG * LANES...  55 us
    unnamed x1, local copies, waits for them, and re-layouts  1.41 us

profile of v4, /device:TPU:0, one launch (start us, length us, event | category | flops | bytes accessed | tf_op | source)
XLA Modules:
  0.0 56.4 jit_solution(7728856575761267296)
XLA Ops:
  0.0 55.0 %filters.1 = f32[192,3072]{1,0:T(8,128)S(1)} custom-call(f32[192,3072]{1,0:T(8,128)} %bitcast.5, f32[1,48]{1,0:T(1,128)} %bitcast.7, f32[24,128]{1,0:T(8,128)} %bitcast.6, f32[48,3072]{1,0:T(8,128)} %dvert.1), custom_call_target="tpu_custom_call" | custom-call | tf_op jit(solution)/shard_map/filters/pallas_call | solution.py:593
  55.0 1.4 %copy.6 = f32[4,48,3072]{2,1,0:T(8,128)} copy(f32[4,48,3072]{2,1,0:T(8,128)S(1)} %bitcast.4) | data formatting | bytes 4718592

commit v5 on v4

--- a/solution.py
+++ b/solution.py
@@ -22,6 +22,8 @@
 NCH = BG * NJ
 CH = 2 * JC * 8
 LAG = 6
+NB = 4
+CB = 22
 IN = 48
 
 
@@ -111,9 +113,9 @@
 
 
 def kernel(ctrl, dlon, dlat, dvert, out, X, Y, Z, PI, PV, OS, DN, DL,
-           SB, RB, RP, CB, SR, SL, FL, FR,
+           SB, RB, RP, RC, SR, SL, FL, FR, WS, WR, OSD, ORC,
            in_sem, pv_sem, dn_sem, dl_sem, s1_sem, r1_sem, s2_sem, r2_sem,
-           sr_sem, sl_sem, fl_sem, fr_sem):
+           sr_sem, sl_sem, fl_sem, fr_sem, ws_sem, os_sem, wr_sem, or_sem):
     lev = lax.axis_index("lev")
     me = lax.axis_index("row")
     barrier = pltpu.get_barrier_semaphore()
@@ -142,18 +144,12 @@
         pl.semaphore_signal(barrier, inc=1, device_id=(lev, lax.rem(me + i + 1, NR)), device_id_type=MESH)
     loop(NR - 1, greet)
 
-    @pl.when(lev > 0)
-    def _():
-        pl.semaphore_signal(barrier, inc=1, device_id=(lev - 1, me), device_id_type=MESH)
-
-    @pl.when(lev < 3)
-    def _():
-        pl.semaphore_signal(barrier, inc=1, device_id=(lev + 1, me), device_id_type=MESH)
+    for step in (1, 3):
+        pl.semaphore_signal(barrier, inc=1, device_id=(lax.rem(lev + step, 4), me), device_id_type=MESH)
 
     zero = jnp.zeros((8, LANES), jnp.float32)
     one = jnp.ones((8, LANES), jnp.float32)
     rest = jnp.zeros((LANES - 96, LANES), jnp.float32)
-    loop(BG * NR, lambda i: SB.__setitem__((pl.ds(pl.multiple_of(i * MSG, 8), 8), slice(None)), zero))
 
     for g in range(2):
         for i in range(96 // IN):
@@ -228,7 +224,7 @@
         return pl.ds(pl.multiple_of((k * ROWS + j) * SEG + bg * 8, 8), 8)
 
     def slot(ref, bg, i):
-        return ref.at[pl.ds(pl.multiple_of((bg * NR + i) * MSG, 8), MSG), :]
+        return ref.at[pl.ds(pl.multiple_of((bg * NR + i) * MSG, 8), 4), :]
 
     def send(src, dst, ssem, rsem, bg):
         def to(i):
@@ -237,11 +233,11 @@
                 src_ref=slot(src, bg, p), dst_ref=slot(dst, bg, me), send_sem=ssem.at[bg],
                 recv_sem=rsem.at[bg], device_id=(lev, p), device_id_type=MESH).start()
         loop(NR - 1, to)
-        at = pl.ds(pl.multiple_of((bg * NR + me) * MSG, 8), MSG)
+        at = pl.ds(pl.multiple_of((bg * NR + me) * MSG, 8), 4)
         dst[at, :] = src[at, :]
 
     def all_of(src, dst, ssem, rsem, bg):
-        at = pl.ds(pl.multiple_of(bg * NR * MSG, 8), (NR - 1) * MSG)
+        at = pl.ds(pl.multiple_of(bg * NR * MSG, 8), (NR - 1) * 4)
         return pltpu.make_async_remote_copy(
             src_ref=src.at[at, :], dst_ref=dst.at[at, :], send_sem=ssem.at[bg], recv_sem=rsem.at[bg],
             device_id=(lev, lax.rem(me + 1, NR)), device_id_type=MESH)
@@ -295,8 +291,7 @@
             for val in range(4):
                 SB[pl.ds((bg * NR + k * 8) * MSG + val, 8, stride=MSG), :] = ends[k][val]
         if bg == 0:
-            neighbours = (lev > 0).astype(jnp.int32) + (lev < 3).astype(jnp.int32)
-            pl.semaphore_wait(barrier, NR - 1 + neighbours)
+            pl.semaphore_wait(barrier, NR - 1 + 2)
         send(SB, RB, s1_sem, r1_sem, bg)
 
     pv_copy.wait()
@@ -326,17 +321,15 @@
         for q in range(NR // 8):
             RP[rows_of(q, 0), :], RP[rows_of(q, 1), :] = states[q]
             RP[rows_of(q, 2), :], RP[rows_of(q, 3), :] = backs[q]
-            for val in range(4, MSG):
-                RP[rows_of(q, val), :] = zero
-        send(RP, CB, s2_sem, r2_sem, bg)
+        send(RP, RC, s2_sem, r2_sem, bg)
 
     def lat_finish(bg):
-        all_of(RP, CB, s2_sem, r2_sem, bg).wait_recv()
+        all_of(RP, RC, s2_sem, r2_sem, bg).wait_recv()
         rl = DL[pl.ds(pl.multiple_of(bg * 8, 8), 8), :]
         g_lat = gain_sq(rl)
 
         def come(k, val):
-            return CB[pl.ds((bg * NR + k * 8) * MSG + val, 8, stride=MSG), :]
+            return RC[pl.ds((bg * NR + k * 8) * MSG + val, 8, stride=MSG), :]
 
         def lat_ahead(i, state):
             xs = [[Z[at_lat(k, i * BLK + q, bg), :] for k in range(LEV)] for q in range(BLK)]
@@ -373,7 +366,7 @@
 
 
     def chunk(ref, c):
-        return ref if c is None else ref.at[pl.ds(pl.multiple_of(c * CH, 8), CH), :]
+        return ref.at[NB * CH:, :] if c is None else ref.at[pl.ds(pl.multiple_of(c * CH, 8), CH), :]
 
     def one_of(sem, c):
         return sem.at[0 if c is None else c]
@@ -387,6 +380,18 @@
         return pltpu.make_async_remote_copy(
             src_ref=chunk(SL, c), dst_ref=chunk(FR, c), send_sem=sl_sem, recv_sem=one_of(fr_sem, c),
             device_id=(lax.rem(lev + 3, 4), me), device_id_type=MESH)
+
+    def four_values(c):
+        at = pl.ds(0, NB * 2 * CH) if c is None else pl.ds(pl.multiple_of(c * 2 * CH, 8), 2 * CH)
+        return pltpu.make_async_remote_copy(
+            src_ref=WS.at[at, :], dst_ref=WR.at[at, :], send_sem=ws_sem, recv_sem=one_of(wr_sem, c),
+            device_id=(lev + 1 - 2 * lax.rem(lev, 2), me), device_id_type=MESH)
+
+    def two_values(c):
+        at = pl.ds(0, NB * CH) if c is None else pl.ds(pl.multiple_of(c * CH, 8), CH)
+        return pltpu.make_async_remote_copy(
+            src_ref=OSD.at[at, :], dst_ref=ORC.at[at, :], send_sem=os_sem, recv_sem=one_of(or_sem, c),
+            device_id=(3 - lev, me), device_id_type=MESH)
 
     def each(c, body):
         bg = c // NJ
@@ -395,8 +400,8 @@
             j = j0 + jj
             rv = PV[pl.ds(bg * 8 * ROWS + j, 8, stride=ROWS), :]
 
-            def at(val, jj=jj):
-                return pl.ds(pl.multiple_of(c * CH + (val * JC + jj) * 8, 8), 8)
+            def at(val, jj=jj, pitch=CH):
+                return pl.ds(pl.multiple_of(c * pitch + (val * JC + jj) * 8, 8), 8)
 
             def zat(k, j=j):
                 return pl.ds(pl.multiple_of((k * ROWS + j) * SEG + bg * 8, 8), 8)
@@ -439,10 +444,24 @@
                         pl.ds(pl.multiple_of((bg * 8 + b) * LANES, LANES), LANES)] = OS[
                             (b * LEV + k) * 8:(b * LEV + k + 1) * 8, :]
 
+    def wide(at, val):
+        return at(val, pitch=2 * CH)
+
+    def moved(rv, first, second):
+        r2 = rv * rv
+        r4 = r2 * r2
+        return r4 * (first + 4.0 * second), r4 * second
+
+    def both(rv, sums3, u, d):
+        e0, e1, e2 = sums3
+        return rv * (e1 * u + e2 * d), rv * (e0 * u + e1 * d)
+
     def ready(c):
         @pl.when(lax.rem(c, NJ) == 0)
         def _():
             lat_finish(c // NJ)
+
+    lat_finish(0)
 
     @pl.when(lev == 0)
     def _():
@@ -457,7 +476,43 @@
                 SR[at(1), :] = d
             each(c, body)
             right(c).start()
-        loop(NCH, first)
+        loop(NCH - NB, lambda c: first(NB + c))
+
+        def inner(c):
+            four_values(c).wait_recv()
+
+            def body(rv, at, zat, put):
+                us, u, d = ahead(rv, [Z[zat(k), :] for k in range(LEV)], None, None)
+                for k in range(LEV):
+                    Z[zat(k), :] = us[k]
+                WS[wide(at, 0), :] = u
+                WS[wide(at, 1), :] = d
+                u, d = moved(rv, u, d)
+                OSD[at(0), :] = u + WR[wide(at, 0), :]
+                OSD[at(1), :] = d + WR[wide(at, 1), :]
+            each(c, body)
+            two_values(c).start()
+        loop(NB, inner)
+
+        def outer(c):
+            two_values(c).wait_recv()
+
+            def body(rv, at, zat, put):
+                q = rv * rv
+                q2 = q * q
+                av, aw = both(rv, sums_double(q, 4.0, q2 * q2, *four(q)), OSD[at(0), :], OSD[at(1), :])
+                v, w = ORC[at(0), :] + av, ORC[at(1), :] + aw
+                WS[wide(at, 2), :] = v
+                WS[wide(at, 3), :] = w
+                v, w = moved(rv, v, w)
+                av, aw = both(rv, four(q), WS[wide(at, 0), :], WS[wide(at, 1), :])
+                v = v + av + WR[wide(at, 2), :]
+                w = w + aw + WR[wide(at, 3), :]
+                vs, _, _ = back(rv, [Z[zat(k), :] for k in range(LEV)], v, w)
+                put(vs)
+            each(c, body)
+            send_out(c)
+        loop(NB, outer)
 
         def second(c):
             left(c).wait_recv()
@@ -467,8 +522,16 @@
                 put(vs)
             each(c, body)
             send_out(c)
-        loop(NCH, second)
-        right(None).wait_send()
+
+        def second_and_rest(i):
+            @pl.when(i == CB)
+            def _():
+                right(None).wait_send()
+                loop(NB, lambda c: four_values(c).start())
+            second(NB + i)
+        loop(NCH - NB, second_and_rest)
+        four_values(None).wait_send()
+        two_values(None).wait_send()
 
     @pl.when(lev == 3)
     def _():
@@ -482,7 +545,39 @@
                 SL[at(1), :] = w
             each(c, body)
             left(c).start()
-        loop(NCH, first)
+        loop(NCH - NB, lambda c: first(NB + c))
+
+        def inner(c):
+            four_values(c).wait_recv()
+
+            def body(rv, at, zat, put):
+                us, _, _ = ahead(rv, [Z[zat(k), :] for k in range(LEV)], None, None)
+                _, v, w = back(rv, us, None, None)
+                av, aw = both(rv, four(rv * rv), WR[wide(at, 0), :], WR[wide(at, 1), :])
+                v, w = moved(rv, v + av, w + aw)
+                OSD[at(0), :] = v + WR[wide(at, 2), :]
+                OSD[at(1), :] = w + WR[wide(at, 3), :]
+            each(c, body)
+            two_values(c).start()
+        loop(NB, inner)
+
+        def outer(c):
+            two_values(c).wait_recv()
+
+            def body(rv, at, zat, put):
+                u, d = ORC[at(0), :], ORC[at(1), :]
+                WS[wide(at, 0), :] = u
+                WS[wide(at, 1), :] = d
+                u, d = moved(rv, u, d)
+                us, _, _ = ahead(rv, [Z[zat(k), :] for k in range(LEV)],
+                                 u + WR[wide(at, 0), :], d + WR[wide(at, 1), :])
+                vs, v, w = back(rv, us, None, None)
+                WS[wide(at, 2), :] = v
+                WS[wide(at, 3), :] = w
+                put(vs)
+            each(c, body)
+            send_out(c)
+        loop(NB, outer)
 
         def second(c):
             right(c).wait_recv()
@@ -493,21 +588,51 @@
                 put(vs)
             each(c, body)
             send_out(c)
-        loop(NCH, second)
-        left(None).wait_send()
+
+        def second_and_rest(i):
+            @pl.when(i == CB)
+            def _():
+                left(None).wait_send()
+                loop(NB, lambda c: four_values(c).start())
+            second(NB + i)
+        loop(NCH - NB, second_and_rest)
+        four_values(None).wait_send()
+        two_values(None).wait_send()
 
     def staged(first, second):
+        def inner(c):
+            def body(rv, at, zat, put):
+                us, u, d = ahead(rv, [Z[zat(k), :] for k in range(LEV)], None, None)
+                _, v, w = back(rv, us, None, None)
+                for val, x in enumerate((u, d, v, w)):
+                    WS[wide(at, val), :] = x
+            each(c, body)
+            four_values(c).start()
+        loop(NB, inner)
+
         def step(i):
             @pl.when(i < NCH)
             def _():
                 first(i)
 
-            @pl.when(i >= LAG)
+            @pl.when(i >= NB + LAG)
             def _():
                 second(i - LAG)
-        loop(NCH + LAG, step)
+        lax.fori_loop(NB, NCH + LAG, lambda i, carry: (step(i), carry)[1], 0)
+
+        def outer(c):
+            four_values(c).wait_recv()
+
+            def body(rv, at, zat, put):
+                us, _, _ = ahead(rv, [Z[zat(k), :] for k in range(LEV)], WR[wide(at, 0), :], WR[wide(at, 1), :])
+                vs, _, _ = back(rv, us, WR[wide(at, 2), :], WR[wide(at, 3), :])
+                put(vs)
+            each(c, body)
+            send_out(c)
+        loop(NB, outer)
         right(None).wait_send()
         left(None).wait_send()
+        four_values(None).wait_send()
 
     @pl.when(lev == 1)
     def _():
@@ -581,7 +706,7 @@
 
     for bg in range(BG):
         all_of(SB, RB, s1_sem, r1_sem, bg).wait_send()
-        all_of(RP, CB, s2_sem, r2_sem, bg).wait_send()
+        all_of(RP, RC, s2_sem, r2_sem, bg).wait_send()
 
 
 def per_device(control, decay_lon, decay_lat, decay_vert):
@@ -606,7 +731,9 @@
             pltpu.VMEM((SEG, LANES), f32),
         ] + [pltpu.VMEM((BG * NR * MSG, LANES), f32)] * 4
         + [pltpu.VMEM((NCH * CH, LANES), f32)] * 4
-        + [dma((LINES // IN,))] + [dma] * 3 + [dma((BG,))] * 4 + [dma] * 2 + [dma((NCH,))] * 2,
+        + [pltpu.VMEM((NB * 2 * CH, LANES), f32)] * 2 + [pltpu.VMEM((NB * CH, LANES), f32)] * 2
+        + [dma((LINES // IN,))] + [dma] * 3 + [dma((BG,))] * 4 + [dma] * 2 + [dma((NCH,))] * 2
+        + [dma] * 2 + [dma((NB,))] * 2,
         compiler_params=pltpu.CompilerParams(
             collective_id=0, has_side_effects=True, vmem_limit_bytes=50 * 1024 * 1024),
         name="filters",

time: 56.5 us -> 53.1 us (0.940)
  Pallas kernels: 55 us -> 51.5 us
    pallas_call x1, Pallas kernels: 55 us -> 51.5 us  [per_device(): pl.pallas_call(kernel, out_shape=jax.ShapeDtypeStruct((LINES, SEG * LANES...]
where the time goes in v5:
time: 53.1 us; the launch traced here: 52.9 us
  Pallas kernels  51.5 us (97%)
  local copies, waits for them, and re-layouts  1.41 us (3%)
    pallas_call x1, Pallas kernels, per_device(): pl.pallas_call(kernel, out_shape=jax.ShapeDtypeStruct((LINES, SEG * LANES...  51.5 us
    unnamed x1, local copies, waits for them, and re-layouts  1.41 us

profile of v5, /device:TPU:0, one launch (start us, length us, event | category | flops | bytes accessed | tf_op | source)
XLA Modules:
  0.0 52.9 jit_solution(6156563896272006843)
XLA Ops:
  0.0 51.5 %filters.1 = f32[192,3072]{1,0:T(8,128)S(1)} custom-call(f32[192,3072]{1,0:T(8,128)} %bitcast.5, f32[1,48]{1,0:T(1,128)} %bitcast.7, f32[24,128]{1,0:T(8,128)} %bitcast.6, f32[48,3072]{1,0:T(8,128)} %dvert.1), custom_call_target="tpu_custom_call" | custom-call | tf_op jit(solution)/shard_map/filters/pallas_call | solution.py:718
  51.5 1.4 %copy.6 = f32[4,48,3072]{2,1,0:T(8,128)} copy(f32[4,48,3072]{2,1,0:T(8,128)S(1)} %bitcast.4) | data formatting | bytes 4718592

commit v6 on v5

--- a/solution.py
+++ b/solution.py
@@ -112,7 +112,7 @@
     return out
 
 
-def kernel(ctrl, dlon, dlat, dvert, out, X, Y, Z, PI, PV, OS, DN, DL,
+def kernel(ctrl, dlon, dlat, dvert, out, X, Y, Z, PI, PV, OS, P1, P2, DN, DL,
            SB, RB, RP, RC, SR, SL, FL, FR, WS, WR, OSD, ORC,
            in_sem, pv_sem, dn_sem, dl_sem, s1_sem, r1_sem, s2_sem, r2_sem,
            sr_sem, sl_sem, fl_sem, fr_sem, ws_sem, os_sem, wr_sem, or_sem):
@@ -167,24 +167,37 @@
     line = jnp.concatenate([line, line, line[:, :32]], axis=1)
     r = jnp.broadcast_to(line, (8, LANES))
     chains = [(g, bg) for g in range(2) for bg in range(BG)]
-    BLK = 4
+    BLK = 8
 
     def at_lon(g, bg, l):
         return pl.ds(pl.multiple_of((g * LANES + l) * SEG + bg * 8, 8), 8)
 
-    def lon_ends(l, state):
+    def at_step(l):
+        return pl.ds(pl.multiple_of(l * 8, 8), 8)
+
+    def lon_ends(i, state):
         p, pp, rest = state
-        new = []
-        for i, (g, bg) in enumerate(chains):
-            u, d, v, w = rest[i]
-            d = r * d + Y[at_lon(g, bg, l), :]
-            u = r * u + d
-            new.append((u, d, v + pp * u, w + p * u))
-        p = r * p
-        return (p, r * pp + p, tuple(new))
+        rest = list(rest)
+        l0 = 2 * i
+        xs = [[Y[at_lon(g, bg, l0 + q), :] for g, bg in chains] for q in range(2)]
+        for q in range(2):
+            P1[at_step(l0 + q), :] = p
+            P2[at_step(l0 + q), :] = pp
+            for k in range(len(chains)):
+                u, d, v, w = rest[k]
+                d = r * d + xs[q][k]
+                u = r * u + d
+                xs[q][k] = u
+                rest[k] = (u, d, v + pp * u, w + p * u)
+            p = r * p
+            pp = r * pp + p
+        for q in range(2):
+            for k, (g, bg) in enumerate(chains):
+                Y[at_lon(g, bg, l0 + q), :] = xs[q][k]
+        return (p, pp, tuple(rest))
 
     init = (one, one, tuple((zero, zero, zero, zero) for _ in chains))
-    _, _, ends = lax.fori_loop(0, LANES, lon_ends, init, unroll=4)
+    _, _, ends = lax.fori_loop(0, LANES // 2, lon_ends, init, unroll=2)
 
     s0, s1, s2 = sums(r * r, 1, 7)
     lon_powers = carry_powers(power(r, 1, 7))
@@ -200,24 +213,6 @@
             ahead_in[g, bg] = states[bg]
             back_in[g, bg] = backs[bg]
 
-    def lon_ahead(i, state):
-        l0 = i * BLK
-        xs = [[Y[at_lon(g, bg, l0 + q), :] for g, bg in chains] for q in range(BLK)]
-        state = list(state)
-        for q in range(BLK):
-            for k in range(len(chains)):
-                u, d = state[k]
-                d = r * d + xs[q][k]
-                u = r * u + d
-                state[k] = (u, d)
-                xs[q][k] = u
-        for q in range(BLK):
-            for k, (g, bg) in enumerate(chains):
-                Y[at_lon(g, bg, l0 + q), :] = xs[q][k]
-        return tuple(state)
-
-    lax.fori_loop(0, LANES // BLK, lon_ahead, tuple(ahead_in[ch] for ch in chains))
-
     g_lon = gain_sq(r)
 
     def at_lat(k, j, bg):
@@ -228,11 +223,11 @@
 
     def send(src, dst, ssem, rsem, bg):
         def to(i):
-            p = lax.rem(me + i + 1, NR)
+            p = lax.rem(me + 11 * (i + 1), NR)
             pltpu.make_async_remote_copy(
                 src_ref=slot(src, bg, p), dst_ref=slot(dst, bg, me), send_sem=ssem.at[bg],
                 recv_sem=rsem.at[bg], device_id=(lev, p), device_id_type=MESH).start()
-        loop(NR - 1, to)
+        loop(NR - 1, to, unroll=8)
         at = pl.ds(pl.multiple_of((bg * NR + me) * MSG, 8), 4)
         dst[at, :] = src[at, :]
 
@@ -243,14 +238,17 @@
             device_id=(lev, lax.rem(me + 1, NR)), device_id_type=MESH)
 
     for bg in range(BG):
-        def lon_back(i, state, bg=bg):
+        came = [(r * u, r * d) for u, d in (ahead_in[0, bg], ahead_in[1, bg])]
+
+        def lon_back(i, state, bg=bg, came=came):
             l0 = LANES - BLK - i * BLK
             xs = [[Y[at_lon(g, bg, l0 + q), :] for g in range(2)] for q in range(BLK)]
+            ps = [(P1[at_step(l0 + q), :], P2[at_step(l0 + q), :]) for q in range(BLK)]
             state = list(state)
             for q in range(BLK - 1, -1, -1):
                 for g in range(2):
                     v, w = state[g]
-                    w = r * w + xs[q][g]
+                    w = r * w + (xs[q][g] + (ps[q][0] * came[g][0] + ps[q][1] * came[g][1]))
                     v = r * v + w
                     state[g] = (v, w)
                     xs[q][g] = v * g_lon
@@ -727,6 +725,8 @@
             pltpu.VMEM((ROWS, SEG * LANES), f32),
             pltpu.VMEM((SEG * ROWS, LANES), f32),
             pltpu.VMEM((8 * LEV * 8, LANES), f32),
+            pltpu.VMEM((8 * LANES, LANES), f32),
+            pltpu.VMEM((8 * LANES, LANES), f32),
             pltpu.VMEM((1, ROWS), f32),
             pltpu.VMEM((SEG, LANES), f32),
         ] + [pltpu.VMEM((BG * NR * MSG, LANES), f32)] * 4

time: 53.1 us -> 52 us (0.979)
  Pallas kernels: 51.5 us -> 50.5 us
    pallas_call x1, Pallas kernels: 51.5 us -> 50.5 us  [per_device(): pl.pallas_call(kernel, out_shape=jax.ShapeDtypeStruct((LINES, SEG * LANES...]
where the time goes in v6:
time: 52 us; the launch traced here: 51.9 us
  Pallas kernels  50.5 us (97%)
  local copies, waits for them, and re-layouts  1.41 us (3%)
    pallas_call x1, Pallas kernels, per_device(): pl.pallas_call(kernel, out_shape=jax.ShapeDtypeStruct((LINES, SEG * LANES...  50.5 us
    unnamed x1, local copies, waits for them, and re-layouts  1.41 us

profile of v6, /device:TPU:0, one launch (start us, length us, event | category | flops | bytes accessed | tf_op | source)
XLA Modules:
  0.0 51.9 jit_solution(3366902292271670241)
XLA Ops:
  0.0 50.5 %filters.1 = f32[192,3072]{1,0:T(8,128)S(1)} custom-call(f32[192,3072]{1,0:T(8,128)} %bitcast.5, f32[1,48]{1,0:T(1,128)} %bitcast.7, f32[24,128]{1,0:T(8,128)} %bitcast.6, f32[48,3072]{1,0:T(8,128)} %dvert.1), custom_call_target="tpu_custom_call" | custom-call | tf_op jit(solution)/shard_map/filters/pallas_call | solution.py:716
  50.5 1.4 %copy.6 = f32[4,48,3072]{2,1,0:T(8,128)} copy(f32[4,48,3072]{2,1,0:T(8,128)S(1)} %bitcast.4) | data formatting | bytes 4718592

commit v7 on v6

--- a/solution.py
+++ b/solution.py
@@ -24,6 +24,7 @@
 LAG = 6
 NB = 4
 CB = 22
+LB = 16
 IN = 48
 
 
@@ -112,7 +113,7 @@
     return out
 
 
-def kernel(ctrl, dlon, dlat, dvert, out, X, Y, Z, PI, PV, OS, P1, P2, DN, DL,
+def kernel(ctrl, dlon, dlat, dvert, out, X, Y, Z, PI, PV, OS, P1, P2, CI, Q1, Q2, DN, DL,
            SB, RB, RP, RC, SR, SL, FL, FR, WS, WR, OSD, ORC,
            in_sem, pv_sem, dn_sem, dl_sem, s1_sem, r1_sem, s2_sem, r2_sem,
            sr_sem, sl_sem, fl_sem, fr_sem, ws_sem, os_sem, wr_sem, or_sem):
@@ -137,15 +138,16 @@
     dn_copy.start()
     for i in range(LINES // IN):
         in_copy(i).start()
+
+    def greet(i):
+        pl.semaphore_signal(barrier, inc=1, device_id=(lev, lax.rem(me + 11 * (i + 1), NR)), device_id_type=MESH)
+    loop(NR - 1, greet, unroll=8)
+
+    for step in (1, 3):
+        pl.semaphore_signal(barrier, inc=1, device_id=(lax.rem(lev + step, 4), me), device_id_type=MESH)
+
     dl_copy.start()
     pv_copy.start()
-
-    def greet(i):
-        pl.semaphore_signal(barrier, inc=1, device_id=(lev, lax.rem(me + i + 1, NR)), device_id_type=MESH)
-    loop(NR - 1, greet)
-
-    for step in (1, 3):
-        pl.semaphore_signal(barrier, inc=1, device_id=(lax.rem(lev + step, 4), me), device_id_type=MESH)
 
     zero = jnp.zeros((8, LANES), jnp.float32)
     one = jnp.ones((8, LANES), jnp.float32)
@@ -202,7 +204,10 @@
     s0, s1, s2 = sums(r * r, 1, 7)
     lon_powers = carry_powers(power(r, 1, 7))
     n = float(LANES)
-    ahead_in, back_in = {}, {}
+
+    def carry_at(g, bg, val):
+        return slice(((g * BG + bg) * 4 + val) * 8, ((g * BG + bg) * 4 + val) * 8 + 8)
+
     for g in range(2):
         of = [ends[g * BG + bg] for bg in range(BG)]
         states = block_carries([e[0] for e in of], [e[1] for e in of], lon_powers, n, False)
@@ -210,10 +215,12 @@
         ws = [e[3] + r * (s0 * u + s1 * d) for e, (u, d) in zip(of, states)]
         backs = block_carries(vs, ws, lon_powers, n, True)
         for bg in range(BG):
-            ahead_in[g, bg] = states[bg]
-            back_in[g, bg] = backs[bg]
+            for val, x in enumerate(states[bg] + backs[bg]):
+                CI[carry_at(g, bg, val), :] = x
 
     g_lon = gain_sq(r)
+    r_pow = [r, r * r, r * r * r, (r * r) * (r * r)]
+    r_lin = [(m + 1.0) * r_pow[m] for m in range(4)]
 
     def at_lat(k, j, bg):
         return pl.ds(pl.multiple_of((k * ROWS + j) * SEG + bg * 8, 8), 8)
@@ -238,26 +245,37 @@
             device_id=(lev, lax.rem(me + 1, NR)), device_id_type=MESH)
 
     for bg in range(BG):
-        came = [(r * u, r * d) for u, d in (ahead_in[0, bg], ahead_in[1, bg])]
+        came = [(r * CI[carry_at(g, bg, 0), :], r * CI[carry_at(g, bg, 1), :]) for g in range(2)]
 
         def lon_back(i, state, bg=bg, came=came):
-            l0 = LANES - BLK - i * BLK
-            xs = [[Y[at_lon(g, bg, l0 + q), :] for g in range(2)] for q in range(BLK)]
-            ps = [(P1[at_step(l0 + q), :], P2[at_step(l0 + q), :]) for q in range(BLK)]
+            l0 = LANES - LB * (i + 1)
+            xs = [[Y[at_lon(g, bg, l0 + q), :] for g in range(2)] for q in range(LB)]
             state = list(state)
-            for q in range(BLK - 1, -1, -1):
+            for top in range(LB - 1, -1, -4):
+                loc = [None, None]
+                for m in range(4):
+                    q = top - m
+                    p, pp = P1[at_step(l0 + q), :], P2[at_step(l0 + q), :]
+                    for g in range(2):
+                        w = xs[q][g] + (p * came[g][0] + pp * came[g][1])
+                        v = w
+                        if m:
+                            w = r * loc[g][1] + w
+                            v = r * loc[g][0] + w
+                        loc[g] = (v, w)
+                        xs[q][g] = v
                 for g in range(2):
                     v, w = state[g]
-                    w = r * w + (xs[q][g] + (ps[q][0] * came[g][0] + ps[q][1] * came[g][1]))
-                    v = r * v + w
-                    state[g] = (v, w)
-                    xs[q][g] = v * g_lon
-            for q in range(BLK):
+                    for m in range(4):
+                        q = top - m
+                        xs[q][g] = xs[q][g] + (r_pow[m] * v + r_lin[m] * w)
+                    state[g] = (xs[top - 3][g], loc[g][1] + r_pow[3] * w)
+            for q in range(LB):
                 for g in range(2):
-                    Y[at_lon(g, bg, l0 + q), :] = xs[q][g]
+                    Y[at_lon(g, bg, l0 + q), :] = xs[q][g] * g_lon
             return tuple(state)
 
-        lax.fori_loop(0, LANES // BLK, lon_back, (back_in[0, bg], back_in[1, bg]), unroll=2)
+        lax.fori_loop(0, LANES // LB, lon_back, tuple((CI[carry_at(g, bg, 2), :], CI[carry_at(g, bg, 3), :]) for g in range(2)))
 
         def turn_out(i, bg=bg):
             for q in range(4):
@@ -272,19 +290,28 @@
             dl_copy.wait()
         rl = DL[bg * 8:(bg + 1) * 8, :]
 
-        def lat_ends(j, state, rl=rl, bg=bg):
+        def lat_ends(i, state, rl=rl, bg=bg):
             p, pp, rest = state
-            new = []
-            for k in range(LEV):
-                u, d, v, w = rest[k]
-                d = rl * d + Z[at_lat(k, j, bg), :]
-                u = rl * u + d
-                new.append((u, d, v + pp * u, w + p * u))
-            p = rl * p
-            return (p, rl * pp + p, tuple(new))
+            rest = list(rest)
+            xs = [[Z[at_lat(k, 4 * i + q, bg), :] for k in range(LEV)] for q in range(4)]
+            for q in range(4):
+                Q1[at_lat(0, 4 * i + q, bg), :] = p
+                Q2[at_lat(0, 4 * i + q, bg), :] = pp
+                for k in range(LEV):
+                    u, d, v, w = rest[k]
+                    d = rl * d + xs[q][k]
+                    u = rl * u + d
+                    xs[q][k] = u
+                    rest[k] = (u, d, v + pp * u, w + p * u)
+                p = rl * p
+                pp = rl * pp + p
+            for q in range(4):
+                for k in range(LEV):
+                    Z[at_lat(k, 4 * i + q, bg), :] = xs[q][k]
+            return (p, pp, tuple(rest))
 
         init = (one, one, tuple((zero, zero, zero, zero) for _ in range(LEV)))
-        _, _, ends = lax.fori_loop(0, ROWS, lat_ends, init, unroll=4)
+        _, _, ends = lax.fori_loop(0, ROWS // 4, lat_ends, init)
         for k in range(LEV):
             for val in range(4):
                 SB[pl.ds((bg * NR + k * 8) * MSG + val, 8, stride=MSG), :] = ends[k][val]
@@ -329,38 +356,25 @@
         def come(k, val):
             return RC[pl.ds((bg * NR + k * 8) * MSG + val, 8, stride=MSG), :]
 
-        def lat_ahead(i, state):
-            xs = [[Z[at_lat(k, i * BLK + q, bg), :] for k in range(LEV)] for q in range(BLK)]
+        came = [(rl * come(k, 0), rl * come(k, 1)) for k in range(LEV)]
+
+        def lat_back(i, state):
+            j0 = ROWS - 4 - i * 4
+            xs = [[Z[at_lat(k, j0 + q, bg), :] for k in range(LEV)] for q in range(4)]
             state = list(state)
-            for q in range(BLK):
-                for k in range(LEV):
-                    u, d = state[k]
-                    d = rl * d + xs[q][k]
-                    u = rl * u + d
-                    state[k] = (u, d)
-                    xs[q][k] = u
-            for q in range(BLK):
-                for k in range(LEV):
-                    Z[at_lat(k, i * BLK + q, bg), :] = xs[q][k]
-            return tuple(state)
-        lax.fori_loop(0, ROWS // BLK, lat_ahead, tuple((come(k, 0), come(k, 1)) for k in range(LEV)))
-
-        def lat_back(i, state):
-            j0 = ROWS - BLK - i * BLK
-            xs = [[Z[at_lat(k, j0 + q, bg), :] for k in range(LEV)] for q in range(BLK)]
-            state = list(state)
-            for q in range(BLK - 1, -1, -1):
+            for q in range(4 - 1, -1, -1):
+                p, pp = Q1[at_lat(0, j0 + q, bg), :], Q2[at_lat(0, j0 + q, bg), :]
                 for k in range(LEV):
                     v, w = state[k]
-                    w = rl * w + xs[q][k]
+                    w = rl * w + (xs[q][k] + (p * came[k][0] + pp * came[k][1]))
                     v = rl * v + w
                     state[k] = (v, w)
                     xs[q][k] = v * g_lat
-            for q in range(BLK):
+            for q in range(4):
                 for k in range(LEV):
                     Z[at_lat(k, j0 + q, bg), :] = xs[q][k]
             return tuple(state)
-        lax.fori_loop(0, ROWS // BLK, lat_back, tuple((come(k, 2), come(k, 3)) for k in range(LEV)))
+        lax.fori_loop(0, ROWS // 4, lat_back, tuple((come(k, 2), come(k, 3)) for k in range(LEV)))
 
 
     def chunk(ref, c):
@@ -369,14 +383,17 @@
     def one_of(sem, c):
         return sem.at[0 if c is None else c]
 
+    def one_from(sem, c):
+        return sem.at[0 if c is None else c - NB]
+
     def right(c):
         return pltpu.make_async_remote_copy(
-            src_ref=chunk(SR, c), dst_ref=chunk(FL, c), send_sem=sr_sem, recv_sem=one_of(fl_sem, c),
+            src_ref=chunk(SR, c), dst_ref=chunk(FL, c), send_sem=sr_sem, recv_sem=one_from(fl_sem, c),
             device_id=(lax.rem(lev + 1, 4), me), device_id_type=MESH)
 
     def left(c):
         return pltpu.make_async_remote_copy(
-            src_ref=chunk(SL, c), dst_ref=chunk(FR, c), send_sem=sl_sem, recv_sem=one_of(fr_sem, c),
+            src_ref=chunk(SL, c), dst_ref=chunk(FR, c), send_sem=sl_sem, recv_sem=one_from(fr_sem, c),
             device_id=(lax.rem(lev + 3, 4), me), device_id_type=MESH)
 
     def four_values(c):
@@ -727,12 +744,15 @@
             pltpu.VMEM((8 * LEV * 8, LANES), f32),
             pltpu.VMEM((8 * LANES, LANES), f32),
             pltpu.VMEM((8 * LANES, LANES), f32),
+            pltpu.VMEM((2 * BG * 4 * 8, LANES), f32),
+            pltpu.VMEM((ROWS * SEG, LANES), f32),
+            pltpu.VMEM((ROWS * SEG, LANES), f32),
             pltpu.VMEM((1, ROWS), f32),
             pltpu.VMEM((SEG, LANES), f32),
         ] + [pltpu.VMEM((BG * NR * MSG, LANES), f32)] * 4
         + [pltpu.VMEM((NCH * CH, LANES), f32)] * 4
         + [pltpu.VMEM((NB * 2 * CH, LANES), f32)] * 2 + [pltpu.VMEM((NB * CH, LANES), f32)] * 2
-        + [dma((LINES // IN,))] + [dma] * 3 + [dma((BG,))] * 4 + [dma] * 2 + [dma((NCH,))] * 2
+        + [dma((LINES // IN,))] + [dma] * 3 + [dma((BG,))] * 4 + [dma] * 2 + [dma((NCH - NB,))] * 2
         + [dma] * 2 + [dma((NB,))] * 2,
         compiler_params=pltpu.CompilerParams(
             collective_id=0, has_side_effects=True, vmem_limit_bytes=50 * 1024 * 1024),

time: 52 us -> 51.9 us (level)
  no operation moved by 1% of the time
where the time goes in v7:
time: 51.9 us; the launch traced here: 51.7 us
  Pallas kernels  50.3 us (97%)
  local copies, waits for them, and re-layouts  1.41 us (3%)
    pallas_call x1, Pallas kernels, per_device(): pl.pallas_call(kernel, out_shape=jax.ShapeDtypeStruct((LINES, SEG * LANES...  50.3 us
    unnamed x1, local copies, waits for them, and re-layouts  1.41 us

profile of v7, /device:TPU:0, one launch (start us, length us, event | category | flops | bytes accessed | tf_op | source)
XLA Modules:
  0.0 51.7 jit_solution(10014170345830173037)
XLA Ops:
  0.0 50.3 %filters.1 = f32[192,3072]{1,0:T(8,128)S(1)} custom-call(f32[192,3072]{1,0:T(8,128)} %bitcast.5, f32[1,48]{1,0:T(1,128)} %bitcast.7, f32[24,128]{1,0:T(8,128)} %bitcast.6, f32[48,3072]{1,0:T(8,128)} %dvert.1), custom_call_target="tpu_custom_call" | custom-call | tf_op jit(solution)/shard_map/filters/pallas_call | solution.py:733
  50.3 1.4 %copy.6 = f32[4,48,3072]{2,1,0:T(8,128)} copy(f32[4,48,3072]{2,1,0:T(8,128)S(1)} %bitcast.4) | data formatting | bytes 4718592

commit v8 on v7

--- a/solution.py
+++ b/solution.py
@@ -199,7 +199,7 @@
         return (p, pp, tuple(rest))
 
     init = (one, one, tuple((zero, zero, zero, zero) for _ in chains))
-    _, _, ends = lax.fori_loop(0, LANES // 2, lon_ends, init, unroll=2)
+    _, _, ends = lax.fori_loop(0, LANES // 2, lon_ends, init, unroll=4)
 
     s0, s1, s2 = sums(r * r, 1, 7)
     lon_powers = carry_powers(power(r, 1, 7))
@@ -234,7 +234,7 @@
             pltpu.make_async_remote_copy(
                 src_ref=slot(src, bg, p), dst_ref=slot(dst, bg, me), send_sem=ssem.at[bg],
                 recv_sem=rsem.at[bg], device_id=(lev, p), device_id_type=MESH).start()
-        loop(NR - 1, to, unroll=8)
+        loop(NR - 1, to, unroll=31)
         at = pl.ds(pl.multiple_of((bg * NR + me) * MSG, 8), 4)
         dst[at, :] = src[at, :]
 
@@ -284,7 +284,7 @@
                     tile = Y[pl.ds(g * LANES * SEG + b, LANES, stride=SEG), :].T
                     for k in range(2):
                         Z[pl.ds((2 * g + k) * ROWS * SEG + b, ROWS, stride=SEG), :] = tile[k * ROWS:(k + 1) * ROWS, :]
-        loop(2, turn_out)
+        loop(2, turn_out, unroll=2)
 
         if bg == 0:
             dl_copy.wait()
@@ -311,7 +311,7 @@
             return (p, pp, tuple(rest))
 
         init = (one, one, tuple((zero, zero, zero, zero) for _ in range(LEV)))
-        _, _, ends = lax.fori_loop(0, ROWS // 4, lat_ends, init)
+        _, _, ends = lax.fori_loop(0, ROWS // 4, lat_ends, init, unroll=2)
         for k in range(LEV):
             for val in range(4):
                 SB[pl.ds((bg * NR + k * 8) * MSG + val, 8, stride=MSG), :] = ends[k][val]

time: 51.9 us -> 51.7 us (level)
  no operation moved by 1% of the time
where the time goes in v8:
time: 51.7 us; the launch traced here: 51.5 us
  Pallas kernels  50.1 us (97%)
  local copies, waits for them, and re-layouts  1.41 us (3%)
    pallas_call x1, Pallas kernels, per_device(): pl.pallas_call(kernel, out_shape=jax.ShapeDtypeStruct((LINES, SEG * LANES...  50.1 us
    unnamed x1, local copies, waits for them, and re-layouts  1.41 us

profile of v8, /device:TPU:0, one launch (start us, length us, event | category | flops | bytes accessed | tf_op | source)
XLA Modules:
  0.0 51.5 jit_solution(1962818539837780101)
XLA Ops:
  0.0 50.1 %filters.1 = f32[192,3072]{1,0:T(8,128)S(1)} custom-call(f32[192,3072]{1,0:T(8,128)} %bitcast.5, f32[1,48]{1,0:T(1,128)} %bitcast.7, f32[24,128]{1,0:T(8,128)} %bitcast.6, f32[48,3072]{1,0:T(8,128)} %dvert.1), custom_call_target="tpu_custom_call" | custom-call | tf_op jit(solution)/shard_map/filters/pallas_call | solution.py:733
  50.1 1.4 %copy.6 = f32[4,48,3072]{2,1,0:T(8,128)} copy(f32[4,48,3072]{2,1,0:T(8,128)S(1)} %bitcast.4) | data formatting | bytes 4718592

commit v9 on v8

--- a/solution.py
+++ b/solution.py
@@ -21,9 +21,9 @@
 NJ = ROWS // JC
 NCH = BG * NJ
 CH = 2 * JC * 8
-LAG = 6
+LAG = 5
 NB = 4
-CB = 22
+CB = 20
 LB = 16
 IN = 48
 

time: 51.7 us -> 51.5 us (level)
  no operation moved by 1% of the time
where the time goes in v9:
time: 51.5 us; the launch traced here: 51.4 us
  Pallas kernels  50 us (97%)
  local copies, waits for them, and re-layouts  1.41 us (3%)
    pallas_call x1, Pallas kernels, per_device(): pl.pallas_call(kernel, out_shape=jax.ShapeDtypeStruct((LINES, SEG * LANES...  50 us
    unnamed x1, local copies, waits for them, and re-layouts  1.41 us

profile of v9, /device:TPU:0, one launch (start us, length us, event | category | flops | bytes accessed | tf_op | source)
XLA Modules:
  0.0 51.4 jit_solution(328364629824456328)
XLA Ops:
  0.0 50.0 %filters.1 = f32[192,3072]{1,0:T(8,128)S(1)} custom-call(f32[192,3072]{1,0:T(8,128)} %bitcast.5, f32[1,48]{1,0:T(1,128)} %bitcast.7, f32[24,128]{1,0:T(8,128)} %bitcast.6, f32[48,3072]{1,0:T(8,128)} %dvert.1), custom_call_target="tpu_custom_call" | custom-call | tf_op jit(solution)/shard_map/filters/pallas_call | solution.py:733
  50.0 1.4 %copy.6 = f32[4,48,3072]{2,1,0:T(8,128)} copy(f32[4,48,3072]{2,1,0:T(8,128)S(1)} %bitcast.4) | data formatting | bytes 4718592
